TPU v7x, 256 devices: a whole 4x4x8 slice. The times are simulated.
256 devices in a mesh: row: 4 (over x_hi, core), col: 4 (over y), layer: 16 (over z, x_lo).
Axes of the slice: x: 4 (x_hi: 2, x_lo: 2; x = x_hi * 2 + x_lo), y: 4, z: 8, core: 2. Of those that a mesh axis runs over, the one named last changes fastest.
Arguments:
- blocks: bfloat16 [16, 4, 64, 12, 4096], P(None, 'col', 'row', None, 'layer'), may hold values from -6 to 6
- grid_class: int32 [64], replicated, may hold values from 0 to 63, each once
- neighbor: int32 [64, 64, 12], replicated, may hold values from 0 to 11, as said below
Outputs:
- updated: bfloat16 [4, 64, 12, 4096], P('col', 'row', None, 'layer')
Inputs may be any that keep to these rules, and one draw needn't show every extreme that they name: `grid_class`: a permutation. neighbor[r, a, m] is the member of class a to which member m of class r is coupled; every block is coupled to exactly one member of each class, and to itself within its own class.
All inputs are finite; a program needn't handle non-finite values.
Results may differ from a plain program's by a relative error of at most 0.007.
Values may be sent and summed in bfloat16 or wider, within the bound.
A program may use at most 128 MiB of HBM per device.

v0:
```python
import math

import jax
import jax.numpy as jnp
from jax import lax
from jax.sharding import PartitionSpec as P

BS = 64
NCLS = 64
WIN = 4


def partial_product(operand_cols, panels_sub, positions, partner_rows, partner_cols, target):
    number = positions.shape[0]
    coupling = jnp.transpose(jnp.take(partner_rows, positions, axis=1), (0, 2, 1))
    offsets = jnp.arange(number, dtype=jnp.int32)[None, None, :]
    chosen = panels_sub[offsets, coupling]
    coupled = jnp.take(partner_cols, positions, axis=0)[offsets, coupling]
    retain = (coupled == target[:, :, None, :]).astype(chosen.dtype)
    chosen = chosen * retain[..., None]
    inner_size = operand_cols.shape[3]
    chosen = chosen.reshape(chosen.shape[:4] + (inner_size, BS))
    return lax.dot_general(
        chosen,
        operand_cols,
        (((2, 4), (2, 3)), ((0, 1), (0, 1))),
        preferred_element_type=jnp.float32,
    )


def multiply(operand, blocks, partner_rows, partner_cols, target):
    operand_all = lax.all_gather(operand, "row", axis=2, tiled=True)
    segment = lax.all_gather(blocks, "col", axis=1, tiled=True)
    heights, number, seg_cols, seg_members, flattened = segment.shape
    positions = (
        jnp.arange(heights, dtype=jnp.int32)[:, None] * WIN
        + jnp.arange(number, dtype=jnp.int32)[None, :]
    ).reshape(-1)
    panels_sub = jnp.transpose(segment, (0, 1, 3, 2, 4)).reshape(
        heights * number, seg_members, seg_cols, flattened
    )
    operand_cols = jnp.take(operand_all, positions, axis=2)
    return partial_product(operand_cols, panels_sub, positions, partner_rows, partner_cols, target)


def per_device(blocks, grid_class, neighbor):
    row_index = lax.axis_index("row")
    col_index = lax.axis_index("col")
    layers = lax.axis_size("layer")
    heights, window_dev, cols_dev, members, flattened = blocks.shape
    inner_size = BS // layers
    scaling = 1.0 / math.sqrt(NCLS * BS)
    partner = neighbor[grid_class[:, None], grid_class[None, :]]
    window_start = col_index * window_dev
    column_start = row_index * cols_dev
    partner_rows = lax.dynamic_slice_in_dim(partner, window_start, window_dev, 0)
    partner_cols = jnp.transpose(
        lax.dynamic_slice_in_dim(partner, column_start, cols_dev, 1), (0, 2, 1)
    )
    target = jnp.transpose(
        lax.dynamic_slice_in_dim(partner_rows, column_start, cols_dev, 1), (0, 2, 1)
    )
    own_rows = blocks[0]
    sectioned = jnp.transpose(
        own_rows.reshape(window_dev, cols_dev, members, inner_size, BS), (0, 2, 1, 4, 3)
    )
    operand = lax.all_to_all(sectioned, "layer", split_axis=3, concat_axis=4, tiled=True)
    first_sum = multiply(operand, blocks, partner_rows, partner_cols, target)
    square = (
        scaling
        * lax.psum_scatter(
            first_sum.astype(jnp.bfloat16), "layer", scatter_dimension=3, tiled=True
        ).astype(jnp.float32)
    ).astype(jnp.bfloat16)
    second_sum = multiply(square, blocks, partner_rows, partner_cols, target)
    cubed = scaling * lax.psum_scatter(
        second_sum.astype(jnp.bfloat16), "layer", scatter_dimension=4, tiled=True
    ).astype(jnp.float32)
    cubed = jnp.transpose(cubed, (0, 2, 1, 4, 3)).reshape(window_dev, cols_dev, members, flattened)
    return (1.5 * own_rows.astype(jnp.float32) - 0.5 * cubed).astype(jnp.bfloat16)


def solution(mesh):
    in_specs = (P(None, "col", "row", None, "layer"), P(), P())
    out_specs = P("col", "row", None, "layer")
    return jax.shard_map(
        per_device, mesh=mesh, in_specs=in_specs, out_specs=out_specs, check_vma=False
    )
```

profile of v0, /device:TPU:1, one launch (start us, length us, event | category | flops | bytes accessed | tf_op | source)
XLA Modules:
  0.0 360.9 jit_solution(4130601382921051038)
XLA Ops:
  6.5 0.7 all-gather.2.cloned.1.call-update
  7.3 0.9 slice.3
  8.2 0.1 reshape_squeeze.3
  8.3 0.6 copy.59
  8.9 0.3 bitcast_bitcast_fusion
  9.2 1.5 reshape.243
  10.7 10.0 %all-to-all-start = ((bf16[16,2,1536]{2,1,0:T(2,128)(2,1)}), bf16[16,2,1536]{2,1,0:T(2,128)(2,1)S(1)}, u32[]{:S(2)}, u32[]{:S(2)}) async-start(bf16[16,2,1536]{2,1,0:T(2,128)(2,1)} %reshape.243), calls=%async_computation | async-start | bytes 196608 | tf_op jit(solution)/shard_map/all_to_all | solution.py:67
  20.9 0.1 reshape.194
  20.9 0.7 copy.54
  21.7 0.1 add.106
  21.8 44.5 %gather_fusion = s32[4096,12]{1,0:T(8,128)} fusion(s32[64,64,12]{2,1,0:T(8,128)S(1)} %copy.54, s32[4096]{0:T(1024)S(1)} %reshape.194), kind=kCustom, calls=%fused_computation.4 | custom fusion | bytes 425984 | tf_op jit(solution)/shard_map/gather | solution.py:53
  66.4 0.8 dynamic-slice_bitcast_fusion
  67.1 0.6 gather_fusion.3
  67.7 0.1 fusion.7
  68.0 1.1 constant_dynamic-slice_fusion
  69.1 0.5 copy.80
  69.6 0.6 gather_fusion.4
  70.2 0.1 broadcast_select_fusion
  70.4 0.1 copy.57
  70.5 0.7 dynamic-slice_bitcast_fusion.1
  71.2 0.1 copy.58
  71.3 5.0 %gather_fusion.2 = s32[768,16]{1,0:T(8,128)S(1)} fusion(s32[64,12,16]{2,0,1:T(8,128)S(1)} %copy.57, s32[768]{0:T(1024)S(1)} %reshape.202), kind=kCustom, calls=%fused_computation.6 | custom fusion | bytes 104448 | tf_op jit(solution)/shard_map/gather | solution.py:18
  76.4 0.5 reshape.244
  77.0 0.2 copy.60
  77.2 0.6 copy.61
  77.8 0.3 copy.62
  78.1 10.8 %all_gather.11 = bf16[1,12,64,4,64]{4,3,2,1,0:T(4,128)(2,1)S(1)} all-gather(bf16[1,12,16,4,64]{4,3,2,1,0:T(4,128)(2,1)S(1)} %copy.62), channel_id=1, replica_groups=mesh['row'=4,'col'=4,'layer'=16] {'row'}, dimensions={2}, use_global_device_ids=true | all-gather | bytes 491520 | tf_op jit(solution)/shard_map/all_gather | solution.py:32
  88.9 1.5 gather_fusion.5
  90.5 0.4 fusion.3
  90.9 9.5 %gather_fusion.1 = bf16[768,16,256]{2,1,0:T(8,128)(2,1)} fusion(bf16[64,12,16,256]{3,2,1,0:T(8,128)(2,1)} %bitcast.83, s32[768]{0:T(1024)S(1)} %reshape.202), kind=kCustom, calls=%fused_computation.5 | custom fusion | bytes 12589056 | tf_op jit(solution)/shard_map/gather | solution.py:17
  100.5 18.7 %gather.26 = bf16[12,64,16,4,64]{4,3,2,1,0:T(4,128)(2,1)} reshape(bf16[768,16,256]{2,1,0:T(8,128)(2,1)} %gather_fusion.1) | data formatting | bytes 12582912 | tf_op jit(solution)/shard_map/gather | solution.py:17
  119.2 17.1 %broadcast_multiply_fusion = bf16[12,64,16,4,64]{4,3,2,1,0:T(4,128)(2,1)} fusion(bf16[12,64,16,4,64]{4,3,2,1,0:T(4,128)(2,1)} %gather.26, bf16[12,64,16]{2,1,0:T(8,128)(2,1)S(1)} %compare_convert_fusion), kind=kLoop, calls=%fused_computation.9 | loop fusion | flops 3145728 | bytes 12607488 | tf_op jit(solution)/shard_map/mul | solution.py:20
  136.3 23.0 %copy.68 = bf16[12,64,16,4,64]{1,4,3,2,0:T(8,128)(2,1)} copy(bf16[12,64,16,4,64]{4,3,2,1,0:T(4,128)(2,1)} %broadcast_multiply_fusion) | data formatting | bytes 12582912 | tf_op jit(solution)/shard_map/mul | solution.py:20
  159.3 7.2 %fusion = bf16[1,12,16,64,64]{4,3,2,1,0:T(8,128)(2,1)S(1)} fusion(bf16[12,64,16,4,64]{1,4,3,2,0:T(8,128)(2,1)} %copy.68, bf16[12,64,4,64,1]{3,2,0,1,4:T(4,128)(2,1)S(1)} %fusion.3), kind=kOutput, calls=%fused_computation.10 | convolution fusion | flops 403439616 | bytes 8257536 | tf_op jit(solution)/shard_map/dot_general | solution.py:23
  166.5 3.7 %copy.65 = bf16[1,12,16,64,64]{4,2,1,0,3:T(8,128)(2,1)} copy(bf16[1,12,16,64,64]{4,3,2,1,0:T(8,128)(2,1)S(1)} %fusion) | data formatting | bytes 3145728 | tf_op jit(solution)/shard_map/convert_element_type | solution.py:72
  170.2 76.3 %reduce-scatter.3.cloned.1.call-done = bf16[1,12,16,4,64]{4,2,1,0,3:T(8,128)(2,1)} async-done(((bf16[1,12,16,64,64]{4,2,1,0,3:T(8,128)(2,1)}), bf16[1,12,16,4,64]{4,2,1,0,3:T(8,128)(2,1)}) %reduce-scatter.3.cloned.1.call-update) | async-done | bytes 98320 | tf_op jit(solution)/shard_map/reduce_scatter | solution.py:71
  246.5 1.0 multiply_convert_fusion
  247.5 16.6 %all_gather.12 = bf16[1,12,64,4,64]{4,2,3,1,0:T(8,128)(2,1)S(1)} all-gather(bf16[1,12,16,4,64]{4,2,3,1,0:T(8,128)(2,1)S(1)} %multiply_convert_fusion), channel_id=1, replica_groups=mesh['row'=4,'col'=4,'layer'=16] {'row'}, dimensions={2}, use_global_device_ids=true | all-gather | bytes 491520 | tf_op jit(solution)/shard_map/all_gather | solution.py:32
  264.1 0.6 copy.67
  264.7 1.5 gather_fusion.6
  266.2 0.4 fusion.2
  266.6 7.2 %fusion.1 = bf16[1,12,16,64,64]{4,3,2,1,0:T(8,128)(2,1)S(1)} fusion(bf16[12,64,16,4,64]{1,4,3,2,0:T(8,128)(2,1)} %copy.68, bf16[12,64,4,64,1]{3,2,0,1,4:T(4,128)(2,1)S(1)} %fusion.2), kind=kOutput, calls=%fused_computation.11 | convolution fusion | flops 403439616 | bytes 8257536 | tf_op jit(solution)/shard_map/dot_general | solution.py:23
  273.9 3.8 %copy.70 = bf16[1,12,16,64,64]{3,2,1,0,4:T(8,128)(2,1)} copy(bf16[1,12,16,64,64]{4,3,2,1,0:T(8,128)(2,1)S(1)} %fusion.1) | data formatting | bytes 3145728 | tf_op jit(solution)/shard_map/convert_element_type | solution.py:77
  277.6 73.7 %reduce-scatter.5.cloned.1.call-done = bf16[1,12,16,64,4]{3,2,1,0,4:T(8,128)(2,1)} async-done(((bf16[1,12,16,64,64]{3,2,1,0,4:T(8,128)(2,1)}), bf16[1,12,16,64,4]{3,2,1,0,4:T(8,128)(2,1)}) %reduce-scatter.5.cloned.1.call-update) | async-done | bytes 98320 | tf_op jit(solution)/shard_map/reduce_scatter | solution.py:76
  351.3 1.0 multiply_bitcast_fusion
  352.3 0.3 copy.71
  352.5 0.3 mul.92
  352.8 1.6 fusion.6
  (24 shorter events, 0.6 us)
Async XLA Ops:
  6.5 14.2 %copy-start.1 = (s32[64]{0:T(128)S(1)}, s32[64]{0:T(128)}, u32[]{:S(2)}) copy-start(s32[64]{0:T(128)} %param.10) | copy-start | bytes 772
  6.5 14.4 %copy-start = (s32[64,64,12]{1,0,2:T(8,128)S(1)}, s32[64,64,12]{1,0,2:T(8,128)}, u32[]{:S(2)}) copy-start(s32[64,64,12]{1,0,2:T(8,128)} %param.11) | copy-start | bytes 589828
  6.5 84.4 %all-gather.2.cloned.1.call-start = ((), (), s32[]{:S(2)}) async-start(), calls=%async_computation.3 | async-start | bytes 7864320 | tf_op jit(solution)/shard_map/all_gather | solution.py:33
  10.7 65.7 %all-to-all-start = ((bf16[16,2,1536]{2,1,0:T(2,128)(2,1)}), bf16[16,2,1536]{2,1,0:T(2,128)(2,1)S(1)}, u32[]{:S(2)}, u32[]{:S(2)}) async-start(bf16[16,2,1536]{2,1,0:T(2,128)(2,1)} %reshape.243), calls=%async_computation | async-start | bytes 196608 | tf_op jit(solution)/shard_map/all_to_all | solution.py:67
  20.7 225.8 %reduce-scatter.3.cloned.1.call-start = ((), (), s32[]{:S(2)}) async-start(), calls=%async_computation.4 | async-start | bytes 3342336 | tf_op jit(solution)/shard_map/reduce_scatter | solution.py:71
  170.2 181.1 %reduce-scatter.5.cloned.1.call-start = ((), (), s32[]{:S(2)}) async-start(), calls=%async_computation.5 | async-start | bytes 3342336 | tf_op jit(solution)/shard_map/reduce_scatter | solution.py:76
Sparse Core Ops, SparseCore 0:
  9.1 71.8 all-gather.1
  170.3 76.1 reduce-scatter.2
  277.8 73.4 reduce-scatter.4
where the time goes:
time: 368 us; the launch traced here: 361 us
  waiting for transfers between devices  151 us (41%)
  local copies, waits for them, and re-layouts  123 us (33%)
  blocking collectives  27.4 us (7%)
  other arithmetic  21.9 us (6%)
  matrix products  14.4 us (4%)
  between operations  13.4 us (4%)
  starting transfers between devices  10.1 us (3%)
    reduce_scatter x1, waiting for transfers between devices, per_device(): lax.psum_scatter(first_sum.astype(jnp.bfloat16), 'layer', scatter_dimensi...  76.3 us
    reduce_scatter x1, waiting for transfers between devices, per_device(): lax.psum_scatter(second_sum.astype(jnp.bfloat16), 'layer', scatter_dimens...  73.7 us
    gather x1, local copies, waits for them, and re-layouts, per_device(): partner = neighbor[grid_class[:, None], grid_class[None, :]]  44.5 us
    gather x2, local copies, waits for them, and re-layouts, partial_product(): chosen = panels_sub[offsets, coupling]  28.3 us
    all_gather x2, blocking collectives, multiply(): operand_all = lax.all_gather(operand, 'row', axis=2, tiled=True)  27.4 us
    mul x1, local copies, waits for them, and re-layouts, partial_product(): chosen = chosen * retain[..., None]  23 us
    mul x1, other arithmetic, partial_product(): chosen = chosen * retain[..., None]  17.1 us
    dot_general x2, matrix products, partial_product(): lax.dot_general(chosen, operand_cols, (((2, 4), (2, 3)), ((0, 1), (0, 1))...  14.4 us
  transfers between devices with their start and end apart: 4, of which 2 were waited for; matrix products, arithmetic and copies ran while one was open for 17% of the time, Pallas kernels for 0%

commit v1 on v0

v1 whole, which is shorter than its diff:
```python
import functools
import math

import jax
import jax.numpy as jnp
from jax import lax
from jax.experimental import pallas as pl
from jax.experimental.pallas import tpu as pltpu
from jax.sharding import PartitionSpec as P

BS = 64
NCLS = 64
WIN = 4
MEM = 12
PAIRS = MEM // 2
NZ = 8
NX = 8
NY = 4
QH = 8
SCALE = 1.0 / math.sqrt(NCLS * BS)
MESH = pl.DeviceIdType.MESH
F32 = jnp.float32
BF16 = jnp.bfloat16
VMEM = pl.BlockSpec(memory_space=pltpu.VMEM)
HBM = pl.BlockSpec(memory_space=pl.ANY)
SMEM = pl.BlockSpec(memory_space=pltpu.SMEM)


def contract(a, b, da, db):
    return lax.dot_general(a, b, (((da,), (db,)), ((), ())), preferred_element_type=F32)


def tables_kernel(gcol_ref, neigh_ref, mu_ref, mask_ref, part_ref, col_ref):
    mine = lax.axis_index("col")
    lanes = lax.broadcasted_iota(jnp.int32, (NCLS, NCLS), 1)
    rows = lax.broadcasted_iota(jnp.int32, (NCLS, NCLS), 0)
    place = (gcol_ref[...] == lanes).astype(F32)
    own_row = contract((lax.broadcasted_iota(jnp.int32, (8, NCLS), 1) == mine).astype(F32), place, 1, 0)[0:1]
    for m in range(MEM):
        table = neigh_ref[m].astype(F32)
        half = contract(place, table, 1, 1)
        col_ref[m] = jnp.sum(half * own_row, axis=1, keepdims=True)
        full = contract(place, half, 1, 1)
        part_ref[m] = full
    row_on = rows == mine
    for m in range(MEM):
        target = jnp.sum(jnp.where(row_on, part_ref[m], 0.0), axis=0, keepdims=True)
        mu_ref[m : m + 1, :] = target.astype(jnp.int32)
        column = col_ref[m]
        coupled = jnp.zeros((NCLS, NCLS), F32)
        for other in range(MEM):
            coupled = jnp.where(column == other, part_ref[other], coupled)
        mask_ref[m] = (coupled == target).astype(F32)


def tables(grid_class, neighbor):
    return pl.pallas_call(
        tables_kernel,
        out_shape=(
            jax.ShapeDtypeStruct((MEM, NCLS), jnp.int32),
            jax.ShapeDtypeStruct((MEM, NCLS, NCLS), F32),
        ),
        in_specs=[VMEM, VMEM],
        out_specs=(VMEM, VMEM),
        scratch_shapes=[pltpu.VMEM((MEM, NCLS, NCLS), F32), pltpu.VMEM((MEM, NCLS, 1), F32)],
    )(grid_class[:, None], jnp.transpose(neighbor, (2, 0, 1)))


def greet(peers):
    barrier = pltpu.get_barrier_semaphore()
    for peer in peers:
        pl.semaphore_signal(barrier, inc=1, device_id=peer, device_id_type=MESH)
    pl.semaphore_wait(barrier, len(peers))


def plane_peers():
    row = lax.axis_index("row")
    layer = lax.axis_index("layer")
    half = lax.rem(layer, 2)
    slot = row * 2 + half
    peers = []
    for offset in range(1, NX):
        other = lax.rem(slot + offset, NX)
        peers.append({"row": other // 2, "layer": layer - half + lax.rem(other, 2)})
    return slot, peers


def gather_kernel(x_ref, y_ref, xg_ref, yg_ref, xsend, xrecv, ysend, yrecv):
    mine = lax.axis_index("col")
    right = {"col": lax.rem(mine + 1, NY)}
    left = {"col": lax.rem(mine + NY - 1, NY)}
    slot, peers = plane_peers()
    greet([right, left] + peers)
    lo, hi = pl.ds(0, 8), pl.ds(8, 8)

    def copy(src, dst, index, peer):
        return pltpu.make_async_remote_copy(
            src_ref=src, dst_ref=dst, send_sem=xsend.at[index], recv_sem=xrecv.at[index],
            device_id=peer, device_id_type=MESH,
        )

    first = [
        copy(x_ref.at[lo], xg_ref.at[0, lo], 0, right),
        copy(x_ref.at[hi], xg_ref.at[1, hi], 1, left),
        copy(x_ref.at[hi], xg_ref.at[0, hi], 2, right),
        copy(x_ref.at[lo], xg_ref.at[1, lo], 3, left),
    ]
    forward = [
        copy(xg_ref.at[0, lo], xg_ref.at[2, lo], 4, right),
        copy(xg_ref.at[1, hi], xg_ref.at[2, hi], 5, left),
    ]
    for one in first:
        one.start()
    sends = []
    for index, peer in enumerate(peers):
        one = pltpu.make_async_remote_copy(
            src_ref=y_ref, dst_ref=yg_ref.at[slot], send_sem=ysend.at[index], recv_sem=yrecv.at[index],
            device_id=peer, device_id_type=MESH,
        )
        one.start()
        sends.append(one)
    yg_ref[slot] = y_ref[...]
    first[0].wait_recv()
    forward[0].start()
    first[1].wait_recv()
    forward[1].start()
    for one in sends:
        one.wait()
    first[0].wait_send()
    first[1].wait_send()
    for one in first[2:] + forward:
        one.wait()


def gather(x, y):
    return pl.pallas_call(
        gather_kernel,
        out_shape=(
            jax.ShapeDtypeStruct((3,) + x.shape, BF16),
            jax.ShapeDtypeStruct((NX,) + y.shape, BF16),
        ),
        in_specs=[HBM, VMEM],
        out_specs=(HBM, VMEM),
        scratch_shapes=[
            pltpu.SemaphoreType.DMA((6,)),
            pltpu.SemaphoreType.DMA((6,)),
            pltpu.SemaphoreType.DMA((NX - 1,)),
            pltpu.SemaphoreType.DMA((NX - 1,)),
        ],
        compiler_params=pltpu.CompilerParams(collective_id=0, has_side_effects=True),
    )(x, y)


def first_kernel(mu_ref, mask_ref, own_ref, xg_ref, y_ref, chosen_ref, out_ref, xs, spread, sems):
    pair = pl.program_id(0)
    mine = lax.axis_index("col")

    @pl.when(pair == 0)
    def _():
        copies = [pltpu.make_async_copy(own_ref, xs.at[mine], sems.at[0])]
        for slot, offset in enumerate((3, 1, 2)):
            copies.append(
                pltpu.make_async_copy(xg_ref.at[slot], xs.at[lax.rem(mine + offset, NY)], sems.at[slot + 1])
            )
        for one in copies:
            one.start()
        for one in copies:
            one.wait()

    base = lax.axis_index("row") * 16 + lax.rem(lax.axis_index("layer"), 2) * QH
    lane = lax.broadcasted_iota(jnp.int32, (NCLS, QH * BS), 1) // BS
    row = lax.broadcasted_iota(jnp.int32, (NCLS, QH * BS), 0)
    expand = (row == lane + base).astype(F32)
    left = y_ref[...].reshape(NCLS * 8, 128).T
    for which in range(2):
        m = pair * 2 + which
        spread[...] = contract(mask_ref[which], expand, 1, 0)

        def step(h, carry):
            for w in range(NY):
                a = h * NY + w
                block = xs[w, h, mu_ref[m, a]].astype(F32)
                kept = block * spread[pl.ds(a, 1), :]
                chosen_ref[which, pl.ds(pl.multiple_of(a * 8, 8), 8), :] = kept.astype(BF16)
            return carry

        lax.fori_loop(0, 16, step, 0)
    top = contract(left[:BS], chosen_ref[0], 1, 0)
    low = contract(left[BS:], chosen_ref[1], 1, 0)
    total = jnp.concatenate([top, low], axis=0).T
    total = total.reshape(QH, NZ, 8, 128)
    for z in range(NZ):
        out_ref[z, 0] = total[:, z].reshape(QH * 8, 128).astype(BF16)


def first_product(mu, mask, own, xg, y):
    return pl.pallas_call(
        first_kernel,
        grid=(PAIRS,),
        out_shape=(
            jax.ShapeDtypeStruct((MEM, NCLS * 8, QH * BS), BF16),
            jax.ShapeDtypeStruct((NZ, PAIRS, QH * 8, 128), BF16),
        ),
        in_specs=[
            SMEM,
            pl.BlockSpec((2, NCLS, NCLS), lambda p: (p, 0, 0)),
            HBM,
            HBM,
            pl.BlockSpec((NX, None, NX * 8, 128), lambda p: (0, p, 0, 0)),
        ],
        out_specs=(
            pl.BlockSpec((2, NCLS * 8, QH * BS), lambda p: (p, 0, 0)),
            pl.BlockSpec((NZ, 1, QH * 8, 128), lambda p: (0, p, 0, 0)),
        ),
        scratch_shapes=[
            pltpu.VMEM((NY, 16, MEM, 8, QH * BS), BF16),
            pltpu.VMEM((NCLS, QH * BS), F32),
            pltpu.SemaphoreType.DMA((4,)),
        ],
    )(mu, mask, own, xg, y)


def second_kernel(chosen_ref, y_ref, out_ref):
    left = y_ref[...].reshape(NCLS * 8, 128).T
    for which in range(2):
        part = contract(left[which * BS : which * BS + BS], chosen_ref[which], 1, 0)
        part = part.reshape(NZ, 2, 4, QH * BS).astype(BF16)
        out_ref[:, :, 0, which] = part


def second_product(chosen, y):
    out = pl.pallas_call(
        second_kernel,
        grid=(PAIRS,),
        out_shape=jax.ShapeDtypeStruct((NZ, 2, PAIRS, 2, 4, QH * BS), BF16),
        in_specs=[
            pl.BlockSpec((2, NCLS * 8, QH * BS), lambda p: (p, 0, 0)),
            pl.BlockSpec((NX, None, NX * 8, 128), lambda p: (0, p, 0, 0)),
        ],
        out_specs=pl.BlockSpec((NZ, 2, 1, 2, 4, QH * BS), lambda p: (0, 0, p, 0, 0, 0)),
    )(chosen, y)
    return out.reshape(NZ * 2, MEM, 4, QH * BS)


def square_kernel(part_ref, yg_ref, held, result, zsend, zrecv, ysend, yrecv):
    layer = lax.axis_index("layer")
    half = lax.rem(layer, 2)
    z = layer // 2
    slot, peers = plane_peers()
    others = [{"layer": lax.rem(z + o, NZ) * 2 + half} for o in range(1, NZ)]
    greet(others + peers)
    sends = []
    for o in (4, 3, 5, 2, 6, 1, 7):
        one = pltpu.make_async_remote_copy(
            src_ref=part_ref.at[lax.rem(z + o, NZ)], dst_ref=held.at[o - 1],
            send_sem=zsend.at[o - 1], recv_sem=zrecv.at[o - 1], device_id=others[o - 1], device_id_type=MESH,
        )
        one.start()
        sends.append(one)
    for one in sends:
        one.wait_recv()
    for p in range(PAIRS):
        total = part_ref[z, p].astype(F32)
        for o in range(NZ - 1):
            total = total + held[o, p].astype(F32)
        result[p] = (SCALE * total).astype(BF16)
    again = []
    for index, peer in enumerate(peers):
        one = pltpu.make_async_remote_copy(
            src_ref=result, dst_ref=yg_ref.at[slot], send_sem=ysend.at[index], recv_sem=yrecv.at[index],
            device_id=peer, device_id_type=MESH,
        )
        one.start()
        again.append(one)
    yg_ref[slot] = result[...]
    for one in sends:
        one.wait_send()
    for one in again:
        one.wait()


def square_sum(part):
    return pl.pallas_call(
        square_kernel,
        out_shape=jax.ShapeDtypeStruct((NX,) + part.shape[1:], BF16),
        in_specs=[VMEM],
        out_specs=VMEM,
        scratch_shapes=[
            pltpu.VMEM((NZ - 1,) + part.shape[1:], BF16),
            pltpu.VMEM(part.shape[1:], BF16),
            pltpu.SemaphoreType.DMA((NZ - 1,)),
            pltpu.SemaphoreType.DMA((NZ - 1,)),
            pltpu.SemaphoreType.DMA((NX - 1,)),
            pltpu.SemaphoreType.DMA((NX - 1,)),
        ],
        compiler_params=pltpu.CompilerParams(collective_id=1, has_side_effects=True),
    )(part)


def cubed_kernel(part_ref, out_ref, held, send, recv):
    layer = lax.axis_index("layer")
    half = lax.rem(layer, 2)
    z = layer // 2
    offsets = [(o, flip) for o in (4, 3, 5, 2, 6, 1, 7, 0) for flip in (1, 0) if o or flip]
    target = {}
    for o, flip in offsets:
        target[o, flip] = lax.rem(z + o, NZ) * 2 + lax.rem(half + flip, 2)
    greet([{"layer": target[key]} for key in offsets])
    sends = []
    for o, flip in offsets:
        index = o * 2 + flip
        one = pltpu.make_async_remote_copy(
            src_ref=part_ref.at[target[o, flip]], dst_ref=held.at[flip, o],
            send_sem=send.at[index], recv_sem=recv.at[index],
            device_id={"layer": target[o, flip]}, device_id_type=MESH,
        )
        one.start()
        sends.append(one)
    for one in sends:
        one.wait_recv()
    for m in range(MEM):
        same = part_ref[layer, m].astype(F32)
        flipped = held[1, 0, m].astype(F32)
        for o in range(1, NZ):
            same = same + held[0, o, m].astype(F32)
            flipped = flipped + held[1, o, m].astype(F32)
        out_ref[half, m] = SCALE * same
        out_ref[1 - half, m] = SCALE * flipped
    for one in sends:
        one.wait_send()


def cubed_sum(part):
    return pl.pallas_call(
        cubed_kernel,
        out_shape=jax.ShapeDtypeStruct((2,) + part.shape[1:], F32),
        in_specs=[VMEM],
        out_specs=VMEM,
        scratch_shapes=[
            pltpu.VMEM((2, NZ) + part.shape[1:], BF16),
            pltpu.SemaphoreType.DMA((2 * NZ,)),
            pltpu.SemaphoreType.DMA((2 * NZ,)),
        ],
        compiler_params=pltpu.CompilerParams(collective_id=2, has_side_effects=True),
    )(part)


def per_device(blocks, grid_class, neighbor):
    heights, window_dev, cols_dev, members, flattened = blocks.shape
    half = lax.rem(lax.axis_index("layer"), 2)
    native = jnp.transpose(blocks[:, 0], (0, 2, 1, 3))
    away = lax.dynamic_slice_in_dim(native, (1 - half) * QH, QH, 2)
    kept = lax.dynamic_slice_in_dim(native, half * QH, QH, 2)
    layers = lax.axis_size("layer")
    came = lax.ppermute(away, "layer", [(l, l ^ 1) for l in range(layers)])
    mu, mask = tables(grid_class, neighbor)

    own = blocks[0, 0]
    cut = own.reshape(2, QH, PAIRS, 2, 4, NZ, 8)
    cut = jnp.transpose(cut, (5, 0, 2, 1, 6, 3, 4)).reshape(layers, PAIRS, QH * 8, 2 * 4)
    cut = lax.all_to_all(cut, "layer", split_axis=0, concat_axis=0, tiled=True)
    cut = cut.reshape(layers, PAIRS, QH * 8, 2, 4)
    left = jnp.transpose(cut, (1, 2, 3, 0, 4)).reshape(PAIRS, QH * 8, 128)

    low = jnp.where(half == 0, kept, came)
    high = jnp.where(half == 0, came, kept)
    both = jnp.stack([low, high], axis=2).reshape(heights, members, 2, QH, 4, BS)
    mine = jnp.transpose(both, (0, 1, 2, 4, 3, 5)).reshape(heights, members, 8, QH * BS)

    xg, yg = gather(mine, left)
    chosen, part = first_product(mu, mask, mine, xg, yg)
    yg = square_sum(part)
    part = second_product(chosen, yg)
    cubed = cubed_sum(part).reshape(2, members, 4, QH, BS)
    cubed = jnp.transpose(cubed, (0, 3, 1, 2, 4)).reshape(cols_dev, members, flattened)
    return (1.5 * own.astype(F32) - 0.5 * cubed).astype(BF16)[None]


def solution(mesh):
    in_specs = (P(None, "col", "row", None, "layer"), P(), P())
    out_specs = P("col", "row", None, "layer")
    return jax.shard_map(
        per_device, mesh=mesh, in_specs=in_specs, out_specs=out_specs, check_vma=False
    )
```

time: 368 us -> 183 us (0.50); the launches traced: 361 us -> 182 us
  waiting for transfers between devices: 151 us -> 3.79 us
  Pallas kernels: 0 us -> 145 us
  local copies, waits for them, and re-layouts: 123 us -> 16.1 us
  blocking collectives: 27.4 us -> 0 us
  other arithmetic: 21.9 us -> 6.68 us
  matrix products: 14.4 us -> 0 us
  between operations: 13.4 us -> 0.18 us
    reduce_scatter x2 -> x0, waiting for transfers between devices: 150 us -> none  [the longest x1 76.3 us: per_device(): lax.psum_scatter(first_sum.astype(jnp.bfloat16), 'layer', scatter_dimensi...]
    pallas_call x0 -> x6, Pallas kernels: none -> 145 us  [the longest x1 61.3 us: gather(): pl.pallas_call(gather_kernel, out_shape=(jax.ShapeDtypeStruct((3,) + x.sh...]
    gather x8 -> x0, local copies, waits for them, and re-layouts: 82.1 us -> none  [the longest x1 44.5 us: per_device(): partner = neighbor[grid_class[:, None], grid_class[None, :]]]
    all_gather x2 -> x0, blocking collectives: 27.4 us -> none  [multiply(): operand_all = lax.all_gather(operand, 'row', axis=2, tiled=True)]
    mul x3, local copies, waits for them, and re-layouts: 23.5 us -> 0.55 us  [per_device(): return (1.5 * own.astype(F32) - 0.5 * cubed).astype(BF16)[None]]
    mul x3 -> x1, other arithmetic: 18 us -> 0.98 us  [per_device(): return (1.5 * own.astype(F32) - 0.5 * cubed).astype(BF16)[None]]
    dot_general x2 -> x0, matrix products: 14.4 us -> none  [partial_product(): lax.dot_general(chosen, operand_cols, (((2, 4), (2, 3)), ((0, 1), (0, 1))...]
    convert_element_type x2 -> x0, local copies, waits for them, and re-layouts: 7.42 us -> none  [the longest x1 3.76 us: per_device(): second_sum.astype(jnp.bfloat16)]
  transfers between devices with their start and end apart: 4 -> 2, of which waited for: 2 -> 1; matrix products, arithmetic and copies ran while one was open for 17% -> 3% of each run, Pallas kernels for 0% -> 2%
where the time goes in v1:
time: 183 us; the launch traced here: 182 us
  Pallas kernels  145 us (79%)
  local copies, waits for them, and re-layouts  16.1 us (9%)
  starting transfers between devices  10.3 us (6%)
  other arithmetic  6.68 us (4%)
  waiting for transfers between devices  3.79 us (2%)
    pallas_call x1, Pallas kernels, gather(): pl.pallas_call(gather_kernel, out_shape=(jax.ShapeDtypeStruct((3,) + x.sh...  61.3 us
    pallas_call x1, Pallas kernels, square_sum(): pl.pallas_call(square_kernel, out_shape=jax.ShapeDtypeStruct((NX,) + part...  35.8 us
    pallas_call x1, Pallas kernels, cubed_sum(): pl.pallas_call(cubed_kernel, out_shape=jax.ShapeDtypeStruct((2,) + part.s...  24.5 us
    pallas_call x1, Pallas kernels, first_product(): pl.pallas_call(first_kernel, grid=(PAIRS,), out_shape=(jax.ShapeDtypeStru...  13.9 us
    all_to_all x1, starting transfers between devices, per_device(): cut = lax.all_to_all(cut, 'layer', split_axis=0, concat_axis=0, tiled=True)  8.3 us
    pallas_call x1, Pallas kernels, second_product(): pl.pallas_call(second_kernel, grid=(PAIRS,), out_shape=jax.ShapeDtypeStru...  6.25 us
    all_to_all x1, waiting for transfers between devices, per_device(): cut = lax.all_to_all(cut, 'layer', split_axis=0, concat_axis=0, tiled=True)  3.79 us
    pallas_call x1, Pallas kernels, tables(): pl.pallas_call(tables_kernel, out_shape=(jax.ShapeDtypeStruct((MEM, NCLS)...  3.67 us
  transfers between devices with their start and end apart: 2, of which 1 were waited for; matrix products, arithmetic and copies ran while one was open for 3% of the time, Pallas kernels for 2%

profile of v1, /device:TPU:1, one launch (start us, length us, event | category | flops | bytes accessed | tf_op | source)
XLA Modules:
  0.0 182.4 jit_solution(12752607074011600648)
XLA Ops:
  0.0 0.0 slice-start
  0.0 2.2 %dynamic-slice_bitcast_fusion = bf16[16,12,8,256]{3,2,1,0:T(8,128)(2,1)} fusion(bf16[16,1,16,12,256]{4,2,3,1,0:T(8,128)(2,1)} %param.3, s32[]{:T(128)S(6)} %select_n.20), kind=kLoop, calls=%fused_computation.4 | loop fusion | bytes 1572868 | tf_op jit(solution)/shard_map/dynamic_slice | solution.py:352
  2.2 2.0 %collective-permute-start = (bf16[16,12,8,256]{3,2,1,0:T(8,128)(2,1)}, bf16[16,12,8,256]{3,2,1,0:T(8,128)(2,1)}, u32[]{:S(2)}, u32[]{:S(2)}) collective-permute-start(bf16[16,12,8,256]{3,2,1,0:T(8,128)(2,1)} %dynamic-slice_bitcast_fusion), channel_id=1, source_target_pairs={{0,1},{1,0},{2,3},{3,2},{4,5},{5,4},{6,7},{7,6},{8,9},{9,8},{10,11... | collective-permute-start | bytes 2359304 | tf_op jit(solution)/shard_map/ppermute | solution.py:355
  4.2 0.0 slice-done
  4.2 1.8 %reshape_squeeze.3 = bf16[2,8,6,2,4,8,8]{6,5,4,1,0,3,2:T(8,128)(2,1)S(1)} reshape(bf16[1,1,16,12,256]{4,2,3,1,0:T(8,128)(2,1)S(1)} %slice-done) | data formatting | bytes 196608 | tf_op jit(solution)/shard_map/reshape;squeeze | solution.py:359
  6.0 0.6 copy.14
  6.7 0.0 copy-start.2
  6.7 1.0 reshape.67
  7.7 0.0 copy-start
  7.7 0.8 reshape.71
  8.5 8.3 %all-to-all-start = ((bf16[16,2,1536]{2,1,0:T(2,128)(2,1)}), bf16[16,2,1536]{2,1,0:T(2,128)(2,1)S(1)}, u32[]{:S(2)}, u32[]{:S(2)}) async-start(bf16[16,2,1536]{2,1,0:T(2,128)(2,1)} %reshape.71), calls=%async_computation | async-start | bytes 196608 | tf_op jit(solution)/shard_map/all_to_all | solution.py:361
  16.8 0.0 copy-done.2
  16.8 0.7 copy.6.gcol_ref
  17.5 3.7 %shard_map.37 = (s32[12,64]{1,0:T(8,128)}, f32[12,64,64]{2,1,0:T(8,128)}) custom-call(s32[64,1]{1,0:T(8,128)} %copy.6.gcol_ref, s32[12,64,64]{2,1,0:T(8,128)} %bitcast.51), custom_call_target="tpu_custom_call" | custom-call | tf_op jit(solution)/shard_map/pallas_call | solution.py:57
  21.2 3.8 %all-to-all-done = bf16[16,2,1536]{2,1,0:T(2,128)(2,1)S(1)} async-done(((bf16[16,2,1536]{2,1,0:T(2,128)(2,1)}), bf16[16,2,1536]{2,1,0:T(2,128)(2,1)S(1)}, u32[]{:S(2)}, u32[]{:S(2)}) %all-to-all-start) | async-done | bytes 98336 | tf_op jit(solution)/shard_map/all_to_all | solution.py:361
  25.0 0.2 reshape.72
  25.1 0.1 copy.9
  25.2 0.1 copy.10
  25.3 0.8 copy.11.y_ref
  26.1 0.0 collective-permute-done
  26.1 0.0 copy-done
  26.1 2.4 %bitcast_select_fusion.1 = (bf16[16,12,8,256]{3,2,1,0:T(8,128)(2,1)S(1)}, bf16[16,12,8,256]{3,2,1,0:T(8,128)(2,1)}) fusion(bf16[16,12,8,256]{3,2,1,0:T(8,128)(2,1)} %collective-permute-done, pred[]{:T(512)S(6)} %eq.4, bf16[16,1,16,12,256]{4,2,3,1,0:T(8,128)(2,1)S(1)} %copy-done, s32[]{:T(128)S(6)} %select_n.19), kind=kLoop, calls=%fused_computation.3 | loop fusion | flops 786432 | bytes 3145733 | tf_op jit(solution)/shard_map/jit(_where)/select_n | solution.py:365
  28.5 0.7 stack.9
  29.1 2.8 %stack.10 = bf16[16,12,1,8,4,64]{5,4,3,1,0,2:T(4,128)(2,1)S(1)} reshape(bf16[16,12,8,256]{3,2,1,0:T(8,128)(2,1)} %get-tuple-element.18) | data formatting | bytes 1572864 | tf_op jit(solution)/shard_map/stack | solution.py:367
  31.9 2.6 %maximum_bitcast_fusion = bf16[16,12,2,4,8,64]{5,3,4,1,0,2:T(4,128)(2,1)S(1)} fusion(bf16[16,12,1,8,4,64]{5,4,3,1,0,2:T(4,128)(2,1)S(1)} %stack.10, bf16[16,12,1,8,4,64]{5,4,3,1,0,2:T(4,128)(2,1)S(1)} %stack.9), kind=kLoop, calls=%fused_computation | loop fusion | flops 786432 | bytes 3145728 | tf_op jit(solution)/shard_map/transpose | solution.py:368
  34.6 1.0 copy.7
  35.5 2.9 %reshape.66.x_ref.own_ref = bf16[16,12,8,512]{3,2,1,0:T(8,128)(2,1)} reshape(bf16[16,12,2,4,8,64]{5,4,3,2,1,0:T(8,128)(2,1)S(1)} %copy.7) | data formatting | bytes 3145728 | tf_op jit(solution)/shard_map/reshape | solution.py:368
  38.4 61.3 %shard_map.38 = (bf16[3,16,12,8,512]{4,3,2,1,0:T(8,128)(2,1)}, bf16[8,6,64,128]{3,2,1,0:T(8,128)(2,1)}) custom-call(bf16[16,12,8,512]{3,2,1,0:T(8,128)(2,1)} %reshape.66.x_ref.own_ref, bf16[6,64,128]{2,1,0:T(8,128)(2,1)} %copy.11.y_ref), custom_call_target="tpu_custom_call" | custom-call | tf_op jit(solution)/shard_map/pallas_call | solution.py:136
  99.7 13.9 %shard_map.39 = (bf16[12,512,512]{2,1,0:T(8,128)(2,1)}, bf16[8,6,64,128]{3,2,1,0:T(8,128)(2,1)}) custom-call(s32[12,64]{1,0:T(8,128)} %get-tuple-element.11.mu_ref, f32[12,64,64]{2,1,0:T(8,128)} %get-tuple-element.12.mask_ref, bf16[16,12,8,512]{3,2,1,0:T(8,128)(2,1)} %reshape.66.x_ref.own_ref, bf16[3,16,12,8,512]{4,3,2,1,0:T(8,128)(2,1)} %get-tuple-element.13.xg_ref, ...), custom_call_target="tpu_custom_call" | custom-call | tf_op jit(solution)/shard_map/pallas_call | solution.py:197
  113.7 35.8 %shard_map.40.y_ref = bf16[8,6,64,128]{3,2,1,0:T(8,128)(2,1)} custom-call(bf16[8,6,64,128]{3,2,1,0:T(8,128)(2,1)} %get-tuple-element.16.part_ref), custom_call_target="tpu_custom_call" | custom-call | tf_op jit(solution)/shard_map/pallas_call | solution.py:283
  149.5 6.3 %shard_map.41 = bf16[8,2,6,2,4,512]{5,4,3,2,1,0:T(4,128)(2,1)} custom-call(bf16[12,512,512]{2,1,0:T(8,128)(2,1)} %get-tuple-element.15.chosen_ref, bf16[8,6,64,128]{3,2,1,0:T(8,128)(2,1)} %shard_map.40.y_ref), custom_call_target="tpu_custom_call" | custom-call | tf_op jit(solution)/shard_map/pallas_call | solution.py:232
  155.7 0.0 copy-start.1
  155.7 24.5 %shard_map.42 = f32[2,12,4,512]{3,2,1,0:T(4,128)} custom-call(bf16[16,12,4,512]{3,2,1,0:T(4,128)(2,1)} %bitcast.45), custom_call_target="tpu_custom_call" | custom-call | tf_op jit(solution)/shard_map/pallas_call | solution.py:334
  180.2 1.0 broadcast_multiply_fusion
  181.2 0.2 mul.51
  181.4 0.1 copy.12
  181.5 0.3 mul.53
  181.7 0.0 copy-done.1
  181.8 0.7 fusion
Async XLA Ops:
  0.0 4.2 %slice-start = ((bf16[16,1,16,12,256]{4,2,3,1,0:T(8,128)(2,1)}), bf16[1,1,16,12,256]{4,2,3,1,0:T(8,128)(2,1)S(1)}, s32[]{:S(2)}) async-start(bf16[16,1,16,12,256]{4,2,3,1,0:T(8,128)(2,1)} %param.3), calls=%async_computation.1 | async-start | bytes 196608 | tf_op jit(solution)/shard_map/slice | solution.py:358
  2.2 23.9 %collective-permute-start = (bf16[16,12,8,256]{3,2,1,0:T(8,128)(2,1)}, bf16[16,12,8,256]{3,2,1,0:T(8,128)(2,1)}, u32[]{:S(2)}, u32[]{:S(2)}) collective-permute-start(bf16[16,12,8,256]{3,2,1,0:T(8,128)(2,1)} %dynamic-slice_bitcast_fusion), channel_id=1, source_target_pairs={{0,1},{1,0},{2,3},{3,2},{4,5},{5,4},{6,7},{7,6},{8,9},{9,8},{10,11... | collective-permute-start | bytes 2359304 | tf_op jit(solution)/shard_map/ppermute | solution.py:355
  6.7 10.2 %copy-start.2 = (s32[64]{0:T(128)S(1)}, s32[64]{0:T(128)}, u32[]{:S(2)}) copy-start(s32[64]{0:T(128)} %param.4) | copy-start | bytes 772
  7.7 18.4 %copy-start = (bf16[16,1,16,12,256]{4,2,3,1,0:T(8,128)(2,1)S(1)}, bf16[16,1,16,12,256]{4,2,3,1,0:T(8,128)(2,1)}, u32[]{:S(2)}) copy-start(bf16[16,1,16,12,256]{4,2,3,1,0:T(8,128)(2,1)} %param.3) | copy-start | bytes 4718596
  8.5 16.5 %all-to-all-start = ((bf16[16,2,1536]{2,1,0:T(2,128)(2,1)}), bf16[16,2,1536]{2,1,0:T(2,128)(2,1)S(1)}, u32[]{:S(2)}, u32[]{:S(2)}) async-start(bf16[16,2,1536]{2,1,0:T(2,128)(2,1)} %reshape.71), calls=%async_computation | async-start | bytes 196608 | tf_op jit(solution)/shard_map/all_to_all | solution.py:361
  155.7 26.0 %copy-start.1 = (bf16[16,1,16,12,256]{4,2,3,1,0:T(8,128)(2,1)S(1)}, bf16[16,1,16,12,256]{4,2,3,1,0:T(8,128)(2,1)}, u32[]{:S(2)}) copy-start(bf16[16,1,16,12,256]{4,2,3,1,0:T(8,128)(2,1)} %param.3) | copy-start | bytes 4718596

commit v2 on v0

v2 whole, which is shorter than its diff:
```python
import functools
import math

import jax
import jax.numpy as jnp
from jax import lax
from jax.experimental import pallas as pl
from jax.experimental.pallas import tpu as pltpu
from jax.sharding import PartitionSpec as P

BS = 64
NCLS = 64
WIN = 4
MEM = 12
PAIRS = MEM // 2
NZ = 8
NX = 8
NY = 4
QH = 8
TILES = 16 * MEM
GROUP = 8
CHUNK = QH * BS // 2
GROUPS = 3
PER = PAIRS // GROUPS
SCALE = 1.0 / math.sqrt(NCLS * BS)
MESH = pl.DeviceIdType.MESH
F32 = jnp.float32
BF16 = jnp.bfloat16
VMEM = pl.BlockSpec(memory_space=pltpu.VMEM)
HBM = pl.BlockSpec(memory_space=pl.ANY)
SMEM = pl.BlockSpec(memory_space=pltpu.SMEM)


def contract(a, b, da, db):
    return lax.dot_general(a, b, (((da,), (db,)), ((), ())), preferred_element_type=F32)


def tables_kernel(gcol_ref, neigh_ref, mu_ref, mask_ref, part_ref, col_ref):
    mine = lax.axis_index("col")
    lanes = lax.broadcasted_iota(jnp.int32, (NCLS, NCLS), 1)
    rows = lax.broadcasted_iota(jnp.int32, (NCLS, NCLS), 0)
    place = (gcol_ref[...] == lanes).astype(F32)
    own_row = contract((lax.broadcasted_iota(jnp.int32, (8, NCLS), 1) == mine).astype(F32), place, 1, 0)[0:1]
    for m in range(MEM):
        table = neigh_ref[m].astype(F32)
        half = contract(place, table, 1, 1)
        col_ref[m] = jnp.sum(half * own_row, axis=1, keepdims=True)
        full = contract(place, half, 1, 1)
        part_ref[m] = full
    row_on = rows == mine
    for m in range(MEM):
        target = jnp.sum(jnp.where(row_on, part_ref[m], 0.0), axis=0, keepdims=True)
        mu_ref[m : m + 1, :] = target.astype(jnp.int32)
        column = col_ref[m]
        coupled = jnp.zeros((NCLS, NCLS), F32)
        for other in range(MEM):
            coupled = jnp.where(column == other, part_ref[other], coupled)
        mask_ref[m] = (coupled == target).astype(F32)


def tables(grid_class, neighbor):
    return pl.pallas_call(
        tables_kernel,
        out_shape=(
            jax.ShapeDtypeStruct((MEM, NCLS), jnp.int32),
            jax.ShapeDtypeStruct((MEM, NCLS, NCLS), F32),
        ),
        in_specs=[VMEM, VMEM],
        out_specs=(VMEM, VMEM),
        scratch_shapes=[pltpu.VMEM((MEM, NCLS, NCLS), F32), pltpu.VMEM((MEM, NCLS, 1), F32)],
    )(grid_class[:, None], jnp.transpose(neighbor, (2, 0, 1)))


def greet(peers):
    barrier = pltpu.get_barrier_semaphore()
    for peer in peers:
        pl.semaphore_signal(barrier, inc=1, device_id=peer, device_id_type=MESH)
    pl.semaphore_wait(barrier, len(peers))


def plane_peers():
    row = lax.axis_index("row")
    layer = lax.axis_index("layer")
    half = lax.rem(layer, 2)
    slot = row * 2 + half
    peers = []
    for offset in range(1, NX):
        other = lax.rem(slot + offset, NX)
        peers.append({"row": other // 2, "layer": layer - half + lax.rem(other, 2)})
    return slot, peers


def whole_kernel(
    mu_ref, mask_ref, kept_ref, came_ref, y_ref, out_ref,
    xs0, xs1, stage, merged, spread, chosen, part, held, result, yg1, yg2, part2, held2,
    xsend, xrecv, y1send, y1recv, zsend, zrecv, y2send, y2recv, csend, crecv,
):
    mine = lax.axis_index("col")
    layer = lax.axis_index("layer")
    half = lax.rem(layer, 2)
    z = layer // 2
    right = {"col": lax.rem(mine + 1, NY)}
    left = {"col": lax.rem(mine + NY - 1, NY)}
    slot, peers = plane_peers()
    below = [{"layer": lax.rem(z + o, NZ) * 2 + half} for o in range(1, NZ)]
    ways = [(o, flip) for o in (4, 3, 5, 2, 6, 1, 7, 0) for flip in (1, 0) if o or flip]
    target = {way: lax.rem(z + way[0], NZ) * 2 + lax.rem(half + way[1], 2) for way in ways}
    greet([right, left] + peers + [{"layer": target[way]} for way in ways])

    xs = (xs0, xs1)
    lo, hi = pl.ds(0, TILES // 2), pl.ds(TILES // 2, TILES // 2)

    def xcopy(chunk, index, src, dst, peer):
        return pltpu.make_async_remote_copy(
            src_ref=src, dst_ref=dst, send_sem=xsend.at[chunk, index], recv_sem=xrecv.at[chunk, index],
            device_id=peer, device_id_type=MESH,
        )

    first, forward = [], []
    for c in range(2):
        ref = xs[c]
        first.append([
            xcopy(c, 0, ref.at[0, lo], ref.at[3, lo], right),
            xcopy(c, 1, ref.at[0, hi], ref.at[1, hi], left),
            xcopy(c, 2, ref.at[0, hi], ref.at[3, hi], right),
            xcopy(c, 3, ref.at[0, lo], ref.at[1, lo], left),
        ])
        forward.append([
            xcopy(c, 4, ref.at[3, lo], ref.at[2, lo], right),
            xcopy(c, 5, ref.at[1, hi], ref.at[2, hi], left),
        ])

    y1 = []
    for index, peer in enumerate(peers):
        one = pltpu.make_async_remote_copy(
            src_ref=y_ref, dst_ref=yg1.at[slot], send_sem=y1send.at[index], recv_sem=y1recv.at[index],
            device_id=peer, device_id_type=MESH,
        )
        one.start()
        y1.append(one)
    yg1[slot] = y_ref[...]

    low_lanes = lax.broadcasted_iota(jnp.int32, (GROUP * 4, 128), 1) < BS

    def relay(block, carry):
        base = block * GROUP
        for t in range(GROUP):
            for source, where in ((kept_ref, half), (came_ref, 1 - half)):
                tile = source[base + t].astype(F32)
                for high in range(2):
                    start = pl.multiple_of(t * 32 + where * 16 + high * 8, 8)
                    stage[pl.ds(start, 8), :] = tile[:, high * 128 : high * 128 + 128]
        for pair in range(QH // 2):
            even = stage[pl.ds(2 * pair, GROUP * 4, stride=8), :]
            odd = stage[pl.ds(2 * pair + 1, GROUP * 4, stride=8), :]
            merged[pair, pl.ds(0, GROUP * 4, stride=2), :] = jnp.where(low_lanes, even, pltpu.roll(odd, BS, 1))
            merged[pair, pl.ds(1, GROUP * 4, stride=2), :] = jnp.where(low_lanes, pltpu.roll(even, BS, 1), odd)
        for pair in range(QH // 2):
            tiles = merged[pair].reshape(GROUP, 8, 128).astype(BF16)
            side = pair % 2 * 128
            xs[pair // 2][0, pl.ds(base, GROUP), :, side : side + 128] = tiles
        return carry

    steps = TILES // GROUP
    lax.fori_loop(0, steps // 2, relay, 0)
    first[0][0].start()
    lax.fori_loop(steps // 2, steps, relay, 0)
    for one in first[0][1:]:
        one.start()

    def pass_on(c):
        first[c][0].wait_recv()
        forward[c][0].start()
        first[c][1].wait_recv()
        forward[c][1].start()

    def arrived(c):
        for one in first[c][2:] + forward[c]:
            one.wait_recv()

    base = lax.axis_index("row") * 16 + half * QH
    slots = [lax.rem(w + NY - mine, NY) for w in range(NY)]

    def multiply(c):
        ref = xs[c]
        lane = lax.broadcasted_iota(jnp.int32, (NCLS, CHUNK), 1) // BS
        row = lax.broadcasted_iota(jnp.int32, (NCLS, CHUNK), 0)
        expand = (row == lane + base + c * (QH // 2)).astype(F32)
        columns = pl.ds(c * CHUNK, CHUNK)

        def one_pair(pair, carry):
            for which in range(2):
                m = pair * 2 + which
                spread[which] = contract(mask_ref[m], expand, 1, 0)

                def select(block, inner):
                    for part_h in range(4):
                        h = block * 4 + part_h
                        for w in range(0, NY, 2):
                            a = h * NY + w
                            both = []
                            for more in range(2):
                                tile = ref[slots[w + more], h * MEM + mu_ref[m, a + more]].astype(F32)
                                both.append(tile * spread[which, pl.ds(a + more, 1), :])
                            rows = pl.ds(pl.multiple_of(a * 8, 16), 16)
                            chosen[m, rows, columns] = jnp.concatenate(both, axis=0).astype(BF16)
                    return inner

                lax.fori_loop(0, 4, select, 0)
            factor = yg1[:, :, pair].reshape(NCLS * 8, 128).T
            top = contract(factor[:BS], chosen[pair * 2, :, columns], 1, 0)
            low = contract(factor[BS:], chosen[pair * 2 + 1, :, columns], 1, 0)
            total = jnp.concatenate([top, low], axis=0).T.reshape(QH // 2, NZ, 8, 128)
            for to in range(NZ):
                part[c, to, pair] = total[:, to].reshape(QH * 4, 128).astype(BF16)
            return carry

        lax.fori_loop(0, PAIRS, one_pair, 0)

    def send_sums(c):
        sends = []
        for o in (4, 3, 5, 2, 6, 1, 7):
            one = pltpu.make_async_remote_copy(
                src_ref=part.at[c, lax.rem(z + o, NZ)], dst_ref=held.at[c, o - 1],
                send_sem=zsend.at[c, o - 1], recv_sem=zrecv.at[c, o - 1], device_id=below[o - 1], device_id_type=MESH,
            )
            one.start()
            sends.append(one)
        return sends

    def add_sums(c, sends):
        for one in sends:
            one.wait_recv()

        def one_pair(pair, carry):
            total = part[c, z, pair].astype(F32)
            for o in range(NZ - 1):
                total = total + held[c, o, pair].astype(F32)
            result[c, pair] = (SCALE * total).astype(BF16)
            return carry

        lax.fori_loop(0, PAIRS, one_pair, 0)
        again = []
        for index, peer in enumerate(peers):
            one = pltpu.make_async_remote_copy(
                src_ref=result.at[c], dst_ref=yg2.at[slot, c], send_sem=y2send.at[c, index],
                recv_sem=y2recv.at[c, index], device_id=peer, device_id_type=MESH,
            )
            one.start()
            again.append(one)
        yg2[slot, c] = result[c]
        return again

    pass_on(0)
    for one in first[1]:
        one.start()
    for one in y1:
        one.wait_recv()
    arrived(0)
    multiply(0)
    sums0 = send_sums(0)
    pass_on(1)
    arrived(1)
    multiply(1)
    sums1 = send_sums(1)
    y20 = add_sums(0, sums0)
    y21 = add_sums(1, sums1)
    for one in y20 + y21:
        one.wait_recv()

    last = []
    for group in range(GROUPS):
        def one_pair(pair, carry):
            factor = yg2[:, :, group * PER + pair].reshape(NCLS * 8, 128).T
            for which in range(2):
                m = (group * PER + pair) * 2 + which
                some = contract(factor[which * BS : which * BS + BS], chosen[m], 1, 0)
                part2[group, :, pair * 2 + which] = some.reshape(NZ * 2, 4, QH * BS).astype(BF16)
            return carry

        lax.fori_loop(0, PER, one_pair, 0)
        for way in ways:
            index = way[0] * 2 + way[1]
            one = pltpu.make_async_remote_copy(
                src_ref=part2.at[group, target[way]], dst_ref=held2.at[group, way[1], way[0]],
                send_sem=csend.at[group, index], recv_sem=crecv.at[group, index],
                device_id={"layer": target[way]}, device_id_type=MESH,
            )
            one.start()
            last.append((group, one))
    for group in range(GROUPS):
        for owner, one in last:
            if owner == group:
                one.wait_recv()

        def add(m, carry):
            same = part2[group, layer, m].astype(F32)
            flipped = held2[group, 1, 0, m].astype(F32)
            for o in range(1, NZ):
                same = same + held2[group, 0, o, m].astype(F32)
                flipped = flipped + held2[group, 1, o, m].astype(F32)
            out_ref[half, group * PER * 2 + m] = SCALE * same
            out_ref[1 - half, group * PER * 2 + m] = SCALE * flipped
            return carry

        lax.fori_loop(0, PER * 2, add, 0)
    for c in range(2):
        for one in first[c] + forward[c]:
            one.wait_send()
    for one in y1 + sums0 + sums1 + y20 + y21:
        one.wait_send()
    for owner, one in last:
        one.wait_send()


def whole(mu, mask, kept, came, y):
    dma = pltpu.SemaphoreType.DMA
    return pl.pallas_call(
        whole_kernel,
        out_shape=jax.ShapeDtypeStruct((2, MEM, 4, QH * BS), F32),
        in_specs=[SMEM, VMEM, VMEM, VMEM, VMEM],
        out_specs=VMEM,
        scratch_shapes=[
            pltpu.VMEM((NY, TILES, 8, CHUNK), BF16),
            pltpu.VMEM((NY, TILES, 8, CHUNK), BF16),
            pltpu.VMEM((GROUP * 32, 128), F32),
            pltpu.VMEM((QH // 2, GROUP * 8, 128), F32),
            pltpu.VMEM((2, NCLS, CHUNK), F32),
            pltpu.VMEM((MEM, NCLS * 8, QH * BS), BF16),
            pltpu.VMEM((2, NZ, PAIRS, QH * 4, 128), BF16),
            pltpu.VMEM((2, NZ - 1, PAIRS, QH * 4, 128), BF16),
            pltpu.VMEM((2, PAIRS, QH * 4, 128), BF16),
            pltpu.VMEM((NX, 2, PAIRS, QH * 4, 128), BF16),
            pltpu.VMEM((NX, 2, PAIRS, QH * 4, 128), BF16),
            pltpu.VMEM((GROUPS, NZ * 2, PER * 2, 4, QH * BS), BF16),
            pltpu.VMEM((GROUPS, 2, NZ, PER * 2, 4, QH * BS), BF16),
            dma((2, 6)),
            dma((2, 6)),
            dma((NX - 1,)),
            dma((NX - 1,)),
            dma((2, NZ - 1)),
            dma((2, NZ - 1)),
            dma((2, NX - 1)),
            dma((2, NX - 1)),
            dma((GROUPS, 2 * NZ)),
            dma((GROUPS, 2 * NZ)),
        ],
        compiler_params=pltpu.CompilerParams(collective_id=0, has_side_effects=True),
    )(mu, mask, kept, came, y)


def per_device(blocks, grid_class, neighbor):
    heights, window_dev, cols_dev, members, flattened = blocks.shape
    half = lax.rem(lax.axis_index("layer"), 2)
    native = jnp.transpose(blocks[:, 0], (0, 2, 1, 3))
    away = lax.dynamic_slice_in_dim(native, (1 - half) * QH, QH, 2)
    kept = lax.dynamic_slice_in_dim(native, half * QH, QH, 2)
    layers = lax.axis_size("layer")
    came = lax.ppermute(away, "layer", [(l, l ^ 1) for l in range(layers)])
    mu, mask = tables(grid_class, neighbor)

    own = blocks[0, 0]
    cut = own.reshape(2, QH, PAIRS, 2, 4, NZ, 8)
    cut = jnp.transpose(cut, (5, 0, 2, 1, 6, 3, 4)).reshape(layers, PAIRS, QH * 8, 2 * 4)
    cut = lax.all_to_all(cut, "layer", split_axis=0, concat_axis=0, tiled=True)
    cut = cut.reshape(layers, PAIRS, 2, QH * 4, 2, 4)
    left = jnp.transpose(cut, (2, 1, 3, 4, 0, 5)).reshape(2, PAIRS, QH * 4, 128)

    cubed = whole(mu, mask, kept.reshape(TILES, QH, 256), came.reshape(TILES, QH, 256), left)
    cubed = cubed.reshape(2, members, 4, QH, BS)
    cubed = jnp.transpose(cubed, (0, 3, 1, 2, 4)).reshape(cols_dev, members, flattened)
    return (1.5 * own.astype(F32) - 0.5 * cubed).astype(BF16)[None]


def solution(mesh):
    in_specs = (P(None, "col", "row", None, "layer"), P(), P())
    out_specs = P("col", "row", None, "layer")
    return jax.shard_map(
        per_device, mesh=mesh, in_specs=in_specs, out_specs=out_specs, check_vma=False
    )
```

time: 368 us -> 140 us (0.38); the launches traced: 361 us -> 139 us
  waiting for transfers between devices: 151 us -> 3.78 us
  Pallas kernels: 0 us -> 114 us
  local copies, waits for them, and re-layouts: 123 us -> 9.5 us
  blocking collectives: 27.4 us -> 0 us
  other arithmetic: 21.9 us -> 1.76 us
  matrix products: 14.4 us -> 0 us
  between operations: 13.4 us -> 0.11 us
    reduce_scatter x2 -> x0, waiting for transfers between devices: 150 us -> none  [the longest x1 76.3 us: per_device(): lax.psum_scatter(first_sum.astype(jnp.bfloat16), 'layer', scatter_dimensi...]
    pallas_call x0 -> x2, Pallas kernels: none -> 114 us  [the longest x1 110 us: whole(): pl.pallas_call(whole_kernel, out_shape=jax.ShapeDtypeStruct((2, MEM, 4, Q...]
    gather x8 -> x0, local copies, waits for them, and re-layouts: 82.1 us -> none  [the longest x1 44.5 us: per_device(): partner = neighbor[grid_class[:, None], grid_class[None, :]]]
    all_gather x2 -> x0, blocking collectives: 27.4 us -> none  [multiply(): operand_all = lax.all_gather(operand, 'row', axis=2, tiled=True)]
    mul x3, local copies, waits for them, and re-layouts: 23.5 us -> 0.55 us  [per_device(): return (1.5 * own.astype(F32) - 0.5 * cubed).astype(BF16)[None]]
    mul x3 -> x1, other arithmetic: 18 us -> 1.1 us  [per_device(): return (1.5 * own.astype(F32) - 0.5 * cubed).astype(BF16)[None]]
    dot_general x2 -> x0, matrix products: 14.4 us -> none  [partial_product(): lax.dot_general(chosen, operand_cols, (((2, 4), (2, 3)), ((0, 1), (0, 1))...]
    convert_element_type x2 -> x0, local copies, waits for them, and re-layouts: 7.42 us -> none  [the longest x1 3.76 us: per_device(): second_sum.astype(jnp.bfloat16)]
  transfers between devices with their start and end apart: 4 -> 2, of which waited for: 2 -> 1; matrix products, arithmetic and copies ran while one was open for 17% -> 4% of each run, Pallas kernels for 0% -> 3%
where the time goes in v2:
time: 140 us; the launch traced here: 139 us
  Pallas kernels  114 us (81%)
  starting transfers between devices  10.3 us (7%)
  local copies, waits for them, and re-layouts  9.5 us (7%)
  waiting for transfers between devices  3.78 us (3%)
  other arithmetic  1.76 us (1%)
    pallas_call x1, Pallas kernels, whole(): pl.pallas_call(whole_kernel, out_shape=jax.ShapeDtypeStruct((2, MEM, 4, Q...  110 us
    all_to_all x1, starting transfers between devices, per_device(): cut = lax.all_to_all(cut, 'layer', split_axis=0, concat_axis=0, tiled=True)  8.29 us
    all_to_all x1, waiting for transfers between devices, per_device(): cut = lax.all_to_all(cut, 'layer', split_axis=0, concat_axis=0, tiled=True)  3.78 us
    pallas_call x1, Pallas kernels, tables(): pl.pallas_call(tables_kernel, out_shape=(jax.ShapeDtypeStruct((MEM, NCLS)...  3.69 us
  transfers between devices with their start and end apart: 2, of which 1 were waited for; matrix products, arithmetic and copies ran while one was open for 4% of the time, Pallas kernels for 3%

profile of v2, /device:TPU:1, one launch (start us, length us, event | category | flops | bytes accessed | tf_op | source)
XLA Modules:
  0.0 139.4 jit_solution(17820060282179907209)
XLA Ops:
  0.0 0.0 slice-start
  0.0 2.7 %dynamic-slice_bitcast_fusion = (bf16[16,12,8,256]{3,2,1,0:T(8,128)(2,1)}, bf16[16,1,8,12,256]{4,2,3,1,0:T(8,128)(2,1)}) fusion(bf16[16,1,16,12,256]{4,2,3,1,0:T(8,128)(2,1)} %param.3, s32[]{:T(128)S(6)} %select_n.7, s32[]{:T(128)S(6)} %select_n.6), kind=kLoop, calls=%fused_computation.1 | loop fusion | bytes 3145736 | tf_op jit(solution)/shard_map/dynamic_slice | solution.py:356
  2.7 2.0 %collective-permute-start = (bf16[16,12,8,256]{3,2,1,0:T(8,128)(2,1)}, bf16[16,12,8,256]{3,2,1,0:T(8,128)(2,1)}, u32[]{:S(2)}, u32[]{:S(2)}) collective-permute-start(bf16[16,12,8,256]{3,2,1,0:T(8,128)(2,1)} %get-tuple-element.9), channel_id=1, source_target_pairs={{0,1},{1,0},{2,3},{3,2},{4,5},{5,4},{6,7},{7,6},{8,9},{9,8},{10,11... | collective-permute-start | bytes 2359304 | tf_op jit(solution)/shard_map/ppermute | solution.py:359
  4.7 0.0 slice-done
  4.7 1.8 %reshape_squeeze.3 = bf16[2,8,6,2,4,8,8]{6,5,4,1,0,3,2:T(8,128)(2,1)S(1)} reshape(bf16[1,1,16,12,256]{4,2,3,1,0:T(8,128)(2,1)S(1)} %slice-done) | data formatting | bytes 196608 | tf_op jit(solution)/shard_map/reshape;squeeze | solution.py:363
  6.5 0.6 copy.12
  7.2 0.0 copy-start.1
  7.2 1.0 reshape.63
  8.2 0.8 reshape.66
  9.0 8.3 %all-to-all-start = ((bf16[16,2,1536]{2,1,0:T(2,128)(2,1)}), bf16[16,2,1536]{2,1,0:T(2,128)(2,1)S(1)}, u32[]{:S(2)}, u32[]{:S(2)}) async-start(bf16[16,2,1536]{2,1,0:T(2,128)(2,1)} %reshape.66), calls=%async_computation | async-start | bytes 196608 | tf_op jit(solution)/shard_map/all_to_all | solution.py:365
  17.3 0.0 copy-done.1
  17.3 0.7 copy.6.gcol_ref
  18.0 3.7 %shard_map.37 = (s32[12,64]{1,0:T(8,128)}, f32[12,64,64]{2,1,0:T(8,128)}) custom-call(s32[64,1]{1,0:T(8,128)} %copy.6.gcol_ref, s32[12,64,64]{2,1,0:T(8,128)} %bitcast.45), custom_call_target="tpu_custom_call" | custom-call | tf_op jit(solution)/shard_map/pallas_call | solution.py:62
  21.7 3.8 %all-to-all-done = bf16[16,2,1536]{2,1,0:T(2,128)(2,1)S(1)} async-done(((bf16[16,2,1536]{2,1,0:T(2,128)(2,1)}), bf16[16,2,1536]{2,1,0:T(2,128)(2,1)S(1)}, u32[]{:S(2)}, u32[]{:S(2)}) %all-to-all-start) | async-done | bytes 98336 | tf_op jit(solution)/shard_map/all_to_all | solution.py:365
  25.5 0.2 reshape.67
  25.6 0.2 reshape.64
  25.8 0.2 copy.8
  26.0 0.8 copy.9.y_ref
  26.8 0.0 collective-permute-done
  26.8 110.3 %shard_map.38 = f32[2,12,4,512]{3,2,1,0:T(4,128)} custom-call(s32[12,64]{1,0:T(8,128)} %get-tuple-element.7.mu_ref, f32[12,64,64]{2,1,0:T(8,128)} %get-tuple-element.8.mask_ref, bf16[192,8,256]{2,1,0:T(8,128)(2,1)} %bitcast.39, bf16[192,8,256]{2,1,0:T(8,128)(2,1)} %bitcast.8.came_ref, bf16[2,6,32,128]{3,2,1,0:T(8,128)(2,1)} %copy.9.y_ref), custom_call_target="tpu_custom_call" | custom-call | tf_op jit(solution)/shard_map/pallas_call | solution.py:318
  137.1 0.0 copy-start
  137.1 1.1 broadcast_multiply_fusion
  138.2 0.2 mul.51
  138.4 0.1 copy.10
  138.5 0.3 mul.53
  138.8 0.0 copy-done
  138.8 0.7 fusion
Async XLA Ops:
  0.0 4.7 %slice-start = ((bf16[16,1,16,12,256]{4,2,3,1,0:T(8,128)(2,1)}), bf16[1,1,16,12,256]{4,2,3,1,0:T(8,128)(2,1)S(1)}, s32[]{:S(2)}) async-start(bf16[16,1,16,12,256]{4,2,3,1,0:T(8,128)(2,1)} %param.3), calls=%async_computation.1 | async-start | bytes 196608 | tf_op jit(solution)/shard_map/slice | solution.py:362
  2.7 24.1 %collective-permute-start = (bf16[16,12,8,256]{3,2,1,0:T(8,128)(2,1)}, bf16[16,12,8,256]{3,2,1,0:T(8,128)(2,1)}, u32[]{:S(2)}, u32[]{:S(2)}) collective-permute-start(bf16[16,12,8,256]{3,2,1,0:T(8,128)(2,1)} %get-tuple-element.9), channel_id=1, source_target_pairs={{0,1},{1,0},{2,3},{3,2},{4,5},{5,4},{6,7},{7,6},{8,9},{9,8},{10,11... | collective-permute-start | bytes 2359304 | tf_op jit(solution)/shard_map/ppermute | solution.py:359
  7.2 10.1 %copy-start.1 = (s32[64]{0:T(128)S(1)}, s32[64]{0:T(128)}, u32[]{:S(2)}) copy-start(s32[64]{0:T(128)} %param.4) | copy-start | bytes 772
  9.0 16.5 %all-to-all-start = ((bf16[16,2,1536]{2,1,0:T(2,128)(2,1)}), bf16[16,2,1536]{2,1,0:T(2,128)(2,1)S(1)}, u32[]{:S(2)}, u32[]{:S(2)}) async-start(bf16[16,2,1536]{2,1,0:T(2,128)(2,1)} %reshape.66), calls=%async_computation | async-start | bytes 196608 | tf_op jit(solution)/shard_map/all_to_all | solution.py:365
  137.1 1.7 %copy-start = (bf16[16,1,16,12,256]{4,2,3,1,0:T(8,128)(2,1)S(1)}, bf16[16,1,16,12,256]{4,2,3,1,0:T(8,128)(2,1)}, u32[]{:S(2)}) copy-start(bf16[16,1,16,12,256]{4,2,3,1,0:T(8,128)(2,1)} %param.3) | copy-start | bytes 4718596

commit v3 on v2

--- a/solution.py
+++ b/solution.py
@@ -19,6 +19,7 @@
 QH = 8
 TILES = 16 * MEM
 GROUP = 8
+PIECE = TILES // 4
 CHUNK = QH * BS // 2
 GROUPS = 3
 PER = PAIRS // GROUPS
@@ -91,9 +92,10 @@
 
 
 def whole_kernel(
-    mu_ref, mask_ref, kept_ref, came_ref, y_ref, out_ref,
-    xs0, xs1, stage, merged, spread, chosen, part, held, result, yg1, yg2, part2, held2,
-    xsend, xrecv, y1send, y1recv, zsend, zrecv, y2send, y2recv, csend, crecv,
+    mu_ref, mask_ref, x_ref, out_ref,
+    own, kept, came, near0, near1, far0, far1, stage, merged, cut, cut_came, cut_stage, factor1,
+    spread, chosen, part, held, result, yg1, yg2, part2, held2,
+    lsem, esend, erecv, asend, arecv, xsend, xrecv, y1send, y1recv, zsend, zrecv, y2send, y2recv, csend, crecv,
 ):
     mine = lax.axis_index("col")
     layer = lax.axis_index("layer")
@@ -105,10 +107,61 @@
     below = [{"layer": lax.rem(z + o, NZ) * 2 + half} for o in range(1, NZ)]
     ways = [(o, flip) for o in (4, 3, 5, 2, 6, 1, 7, 0) for flip in (1, 0) if o or flip]
     target = {way: lax.rem(z + way[0], NZ) * 2 + lax.rem(half + way[1], 2) for way in ways}
+
+    keep = pl.ds(pl.multiple_of(half * QH, QH), QH)
+    away = pl.ds(pl.multiple_of((1 - half) * QH, QH), QH)
+    local = [
+        pltpu.make_async_copy(x_ref.at[pl.ds(0, MEM)], own, lsem.at[0]),
+        pltpu.make_async_copy(x_ref.at[:, keep], kept, lsem.at[1]),
+    ]
+    for one in local:
+        one.start()
     greet([right, left] + peers + [{"layer": target[way]} for way in ways])
 
-    xs = (xs0, xs1)
-    lo, hi = pl.ds(0, TILES // 2), pl.ds(TILES // 2, TILES // 2)
+    pieces = [pl.ds(i * PIECE, PIECE) for i in range(4)]
+    swap = []
+    for i in range(4):
+        one = pltpu.make_async_remote_copy(
+            src_ref=x_ref.at[pieces[i], away], dst_ref=came.at[pieces[i]], send_sem=esend.at[i], recv_sem=erecv.at[i],
+            device_id={"layer": target[0, 1]}, device_id_type=MESH,
+        )
+        one.start()
+        swap.append(one)
+
+    local[0].wait()
+    rows = own[...].reshape(MEM * 16, 256)
+    lane = lax.broadcasted_iota(jnp.int32, (256, 256), 1)
+    apart = lax.broadcasted_iota(jnp.int32, (256, 256), 0) - lane // 128 * 8 - lane % 8
+    line = lax.broadcasted_iota(jnp.int32, (MEM * 16, 256), 0)
+    spot = lax.broadcasted_iota(jnp.int32, (MEM * 16, 256), 1)
+    fits = (spot % 128 // 8 == line // 16 % 2 * 8 + line % 8).astype(F32)
+    wide = lax.broadcasted_iota(jnp.int32, (16, MEM * 16), 1)
+    tall = lax.broadcasted_iota(jnp.int32, (16, MEM * 16), 0)
+    gathers = (tall == wide % 16 // 8 * 8 + wide // 32).astype(BF16)
+
+    def cut_step(step, carry):
+        row4, zpair = step // 4, step % 4
+        pick = (apart == row4 * 64 + zpair * 16).astype(BF16)
+        spread_out = contract(rows, pick, 1, 0) * fits
+        flat = contract(gathers, spread_out.astype(BF16), 1, 0).astype(BF16)
+        for odd in range(2):
+            for side in range(2):
+                cut[(zpair * 2 + odd) * 2 + side, row4] = flat[side * 8 : side * 8 + 8, odd * 128 : odd * 128 + 128]
+        return carry
+
+    lax.fori_loop(0, 16, cut_step, 0)
+    cuts = []
+    for way in ways:
+        index = way[0] * 2 + way[1]
+        one = pltpu.make_async_remote_copy(
+            src_ref=cut.at[target[way]], dst_ref=cut_came.at[layer], send_sem=asend.at[index], recv_sem=arecv.at[index],
+            device_id={"layer": target[way]}, device_id_type=MESH,
+        )
+        one.start()
+        cuts.append(one)
+    cut_came[layer] = cut[layer]
+
+    near, far = (near0, near1), (far0, far1)
 
     def xcopy(chunk, index, src, dst, peer):
         return pltpu.make_async_remote_copy(
@@ -116,36 +169,22 @@
             device_id=peer, device_id_type=MESH,
         )
 
-    first, forward = [], []
+    rightward, leftward, forward = [], [], []
     for c in range(2):
-        ref = xs[c]
-        first.append([
-            xcopy(c, 0, ref.at[0, lo], ref.at[3, lo], right),
-            xcopy(c, 1, ref.at[0, hi], ref.at[1, hi], left),
-            xcopy(c, 2, ref.at[0, hi], ref.at[3, hi], right),
-            xcopy(c, 3, ref.at[0, lo], ref.at[1, lo], left),
-        ])
-        forward.append([
-            xcopy(c, 4, ref.at[3, lo], ref.at[2, lo], right),
-            xcopy(c, 5, ref.at[1, hi], ref.at[2, hi], left),
-        ])
-
-    y1 = []
-    for index, peer in enumerate(peers):
-        one = pltpu.make_async_remote_copy(
-            src_ref=y_ref, dst_ref=yg1.at[slot], send_sem=y1send.at[index], recv_sem=y1recv.at[index],
-            device_id=peer, device_id_type=MESH,
+        ref = near[c]
+        rightward.append([xcopy(c, i, ref.at[0, pieces[i]], ref.at[2, pieces[i]], right) for i in range(4)])
+        leftward.append([xcopy(c, 4 + i, ref.at[0, pieces[i]], ref.at[1, pieces[i]], left) for i in range(4)])
+        forward.append(
+            [xcopy(c, 8 + i, ref.at[2, pieces[i]], far[c].at[pieces[i]], right) for i in range(2)]
+            + [xcopy(c, 8 + i, ref.at[1, pieces[i]], far[c].at[pieces[i]], left) for i in range(2, 4)]
         )
-        one.start()
-        y1.append(one)
-    yg1[slot] = y_ref[...]
 
     low_lanes = lax.broadcasted_iota(jnp.int32, (GROUP * 4, 128), 1) < BS
 
     def relay(block, carry):
         base = block * GROUP
         for t in range(GROUP):
-            for source, where in ((kept_ref, half), (came_ref, 1 - half)):
+            for source, where in ((kept, half), (came, 1 - half)):
                 tile = source[base + t].astype(F32)
                 for high in range(2):
                     start = pl.multiple_of(t * 32 + where * 16 + high * 8, 8)
@@ -158,61 +197,87 @@
         for pair in range(QH // 2):
             tiles = merged[pair].reshape(GROUP, 8, 128).astype(BF16)
             side = pair % 2 * 128
-            xs[pair // 2][0, pl.ds(base, GROUP), :, side : side + 128] = tiles
+            near[pair // 2][0, pl.ds(base, GROUP), :, side : side + 128] = tiles
         return carry
 
-    steps = TILES // GROUP
-    lax.fori_loop(0, steps // 2, relay, 0)
-    first[0][0].start()
-    lax.fori_loop(steps // 2, steps, relay, 0)
-    for one in first[0][1:]:
+    local[1].wait()
+    for i in range(4):
+        swap[i].wait_recv()
+        lax.fori_loop(i * (PIECE // GROUP), (i + 1) * (PIECE // GROUP), relay, 0)
+        rightward[0][i].start()
+        leftward[0][i].start()
+
+    for one in cuts:
+        one.wait_recv()
+    cut_stage[...] = cut_came[...].astype(F32).reshape(NZ * 64, 128)
+    for p in range(PAIRS):
+        turned = cut_stage[pl.ds(p, BS, stride=8), :].T
+        both = jnp.concatenate([turned[:BS], turned[BS:]], axis=1).astype(BF16)
+        for q in range(QH):
+            away_by = lax.rem(q % 4 + NY - mine, NY)
+            place = away_by + away_by // 2 * (5 - 2 * away_by)
+            factor1[q // 4, place, p] = both[q * 8 : q * 8 + 8]
+    y1 = []
+    for index, peer in enumerate(peers):
+        one = pltpu.make_async_remote_copy(
+            src_ref=factor1, dst_ref=yg1.at[slot], send_sem=y1send.at[index], recv_sem=y1recv.at[index],
+            device_id=peer, device_id_type=MESH,
+        )
         one.start()
-
-    def pass_on(c):
-        first[c][0].wait_recv()
-        forward[c][0].start()
-        first[c][1].wait_recv()
-        forward[c][1].start()
-
-    def arrived(c):
-        for one in first[c][2:] + forward[c]:
-            one.wait_recv()
+        y1.append(one)
+    yg1[slot] = factor1[...]
 
     base = lax.axis_index("row") * 16 + half * QH
-    slots = [lax.rem(w + NY - mine, NY) for w in range(NY)]
-
-    def multiply(c):
-        ref = xs[c]
+    order = [lax.rem(mine + d, NY) for d in (0, 1, 3, 2)]
+
+    def select(c, e, m, block, count, ref):
+        columns = pl.ds(c * CHUNK, CHUNK)
+        for pair_h in range(0, count, 2):
+            h = block * count + pair_h
+            both = []
+            for more in range(2):
+                a = (h + more) * NY + order[e]
+                tile = ref[(h + more) * MEM + mu_ref[m, a]].astype(F32)
+                both.append(tile * spread[m, pl.ds(a, 1), :])
+            at = pl.ds(pl.multiple_of(e * 128 + h * 8, 16), 16)
+            chosen[m, at, columns] = jnp.concatenate(both, axis=0).astype(BF16)
+
+    def select_near(c):
         lane = lax.broadcasted_iota(jnp.int32, (NCLS, CHUNK), 1) // BS
         row = lax.broadcasted_iota(jnp.int32, (NCLS, CHUNK), 0)
         expand = (row == lane + base + c * (QH // 2)).astype(F32)
+
+        def one_member(m, carry):
+            spread[m] = contract(mask_ref[m], expand, 1, 0)
+
+            def some(block, inner):
+                for e in range(3):
+                    select(c, e, m, block, 4, near[c].at[e])
+                return inner
+
+            return lax.fori_loop(0, 4, some, carry)
+
+        lax.fori_loop(0, MEM, one_member, 0)
+
+    def factor_of(ref, pair):
+        return jnp.concatenate([ref[:, :, e, pair].reshape(128, 128) for e in range(4)], axis=0).T
+
+    def multiply(c):
         columns = pl.ds(c * CHUNK, CHUNK)
 
         def one_pair(pair, carry):
             for which in range(2):
-                m = pair * 2 + which
-                spread[which] = contract(mask_ref[m], expand, 1, 0)
-
-                def select(block, inner):
-                    for part_h in range(4):
-                        h = block * 4 + part_h
-                        for w in range(0, NY, 2):
-                            a = h * NY + w
-                            both = []
-                            for more in range(2):
-                                tile = ref[slots[w + more], h * MEM + mu_ref[m, a + more]].astype(F32)
-                                both.append(tile * spread[which, pl.ds(a + more, 1), :])
-                            rows = pl.ds(pl.multiple_of(a * 8, 16), 16)
-                            chosen[m, rows, columns] = jnp.concatenate(both, axis=0).astype(BF16)
+                def some(block, inner):
+                    select(c, 3, pair * 2 + which, block, 8, far[c])
                     return inner
 
-                lax.fori_loop(0, 4, select, 0)
-            factor = yg1[:, :, pair].reshape(NCLS * 8, 128).T
+                lax.fori_loop(0, 2, some, 0)
+            factor = factor_of(yg1, pair)
             top = contract(factor[:BS], chosen[pair * 2, :, columns], 1, 0)
             low = contract(factor[BS:], chosen[pair * 2 + 1, :, columns], 1, 0)
             total = jnp.concatenate([top, low], axis=0).T.reshape(QH // 2, NZ, 8, 128)
             for to in range(NZ):
-                part[c, to, pair] = total[:, to].reshape(QH * 4, 128).astype(BF16)
+                part[c, to, pair] = total[:, to].astype(BF16)
             return carry
 
         lax.fori_loop(0, PAIRS, one_pair, 0)
@@ -233,10 +298,11 @@
             one.wait_recv()
 
         def one_pair(pair, carry):
-            total = part[c, z, pair].astype(F32)
-            for o in range(NZ - 1):
-                total = total + held[c, o, pair].astype(F32)
-            result[c, pair] = (SCALE * total).astype(BF16)
+            for e in range(4):
+                total = part[c, z, pair, order[e]].astype(F32)
+                for o in range(NZ - 1):
+                    total = total + held[c, o, pair, order[e]].astype(F32)
+                result[c, e, pair] = (SCALE * total).astype(BF16)
             return carry
 
         lax.fori_loop(0, PAIRS, one_pair, 0)
@@ -251,16 +317,37 @@
         yg2[slot, c] = result[c]
         return again
 
+    def pass_on(c):
+        for i in range(2):
+            rightward[c][i].wait_recv()
+            forward[c][i].start()
+        for i in range(2, 4):
+            leftward[c][i].wait_recv()
+            forward[c][i].start()
+
+    def near_arrived(c):
+        for one in leftward[c][:2] + rightward[c][2:]:
+            one.wait_recv()
+
+    def far_arrived(c):
+        for one in forward[c]:
+            one.wait_recv()
+
     pass_on(0)
-    for one in first[1]:
-        one.start()
+    for i in range(4):
+        rightward[1][i].start()
+        leftward[1][i].start()
+    near_arrived(0)
+    select_near(0)
     for one in y1:
         one.wait_recv()
-    arrived(0)
+    far_arrived(0)
     multiply(0)
     sums0 = send_sums(0)
     pass_on(1)
-    arrived(1)
+    near_arrived(1)
+    select_near(1)
+    far_arrived(1)
     multiply(1)
     sums1 = send_sums(1)
     y20 = add_sums(0, sums0)
@@ -271,7 +358,7 @@
     last = []
     for group in range(GROUPS):
         def one_pair(pair, carry):
-            factor = yg2[:, :, group * PER + pair].reshape(NCLS * 8, 128).T
+            factor = factor_of(yg2, group * PER + pair)
             for which in range(2):
                 m = (group * PER + pair) * 2 + which
                 some = contract(factor[which * BS : which * BS + BS], chosen[m], 1, 0)
@@ -305,37 +392,52 @@
 
         lax.fori_loop(0, PER * 2, add, 0)
     for c in range(2):
-        for one in first[c] + forward[c]:
+        for one in rightward[c] + leftward[c] + forward[c]:
             one.wait_send()
-    for one in y1 + sums0 + sums1 + y20 + y21:
+    for one in swap + cuts + y1 + sums0 + sums1 + y20 + y21:
         one.wait_send()
     for owner, one in last:
         one.wait_send()
 
 
-def whole(mu, mask, kept, came, y):
+def whole(mu, mask, x):
     dma = pltpu.SemaphoreType.DMA
+    square = (4, PAIRS, 8, 128)
     return pl.pallas_call(
         whole_kernel,
         out_shape=jax.ShapeDtypeStruct((2, MEM, 4, QH * BS), F32),
-        in_specs=[SMEM, VMEM, VMEM, VMEM, VMEM],
+        in_specs=[SMEM, VMEM, HBM],
         out_specs=VMEM,
         scratch_shapes=[
-            pltpu.VMEM((NY, TILES, 8, CHUNK), BF16),
-            pltpu.VMEM((NY, TILES, 8, CHUNK), BF16),
+            pltpu.VMEM((MEM, 16, 256), BF16),
+            pltpu.VMEM((TILES, QH, 256), BF16),
+            pltpu.VMEM((TILES, QH, 256), BF16),
+            pltpu.VMEM((3, TILES, 8, CHUNK), BF16),
+            pltpu.VMEM((3, TILES, 8, CHUNK), BF16),
+            pltpu.VMEM((TILES, 8, CHUNK), BF16),
+            pltpu.VMEM((TILES, 8, CHUNK), BF16),
             pltpu.VMEM((GROUP * 32, 128), F32),
             pltpu.VMEM((QH // 2, GROUP * 8, 128), F32),
-            pltpu.VMEM((2, NCLS, CHUNK), F32),
+            pltpu.VMEM((NZ * 2, 4, 8, 128), BF16),
+            pltpu.VMEM((NZ * 2, 4, 8, 128), BF16),
+            pltpu.VMEM((NZ * 64, 128), F32),
+            pltpu.VMEM((2,) + square, BF16),
+            pltpu.VMEM((MEM, NCLS, CHUNK), F32),
             pltpu.VMEM((MEM, NCLS * 8, QH * BS), BF16),
-            pltpu.VMEM((2, NZ, PAIRS, QH * 4, 128), BF16),
-            pltpu.VMEM((2, NZ - 1, PAIRS, QH * 4, 128), BF16),
-            pltpu.VMEM((2, PAIRS, QH * 4, 128), BF16),
-            pltpu.VMEM((NX, 2, PAIRS, QH * 4, 128), BF16),
-            pltpu.VMEM((NX, 2, PAIRS, QH * 4, 128), BF16),
+            pltpu.VMEM((2, NZ, PAIRS, QH // 2, 8, 128), BF16),
+            pltpu.VMEM((2, NZ - 1, PAIRS, QH // 2, 8, 128), BF16),
+            pltpu.VMEM((2,) + square, BF16),
+            pltpu.VMEM((NX, 2) + square, BF16),
+            pltpu.VMEM((NX, 2) + square, BF16),
             pltpu.VMEM((GROUPS, NZ * 2, PER * 2, 4, QH * BS), BF16),
             pltpu.VMEM((GROUPS, 2, NZ, PER * 2, 4, QH * BS), BF16),
-            dma((2, 6)),
-            dma((2, 6)),
+            dma((2,)),
+            dma((4,)),
+            dma((4,)),
+            dma((NZ * 2,)),
+            dma((NZ * 2,)),
+            dma((2, 12)),
+            dma((2, 12)),
             dma((NX - 1,)),
             dma((NX - 1,)),
             dma((2, NZ - 1)),
@@ -346,30 +448,16 @@
             dma((GROUPS, 2 * NZ)),
         ],
         compiler_params=pltpu.CompilerParams(collective_id=0, has_side_effects=True),
-    )(mu, mask, kept, came, y)
+    )(mu, mask, x)
 
 
 def per_device(blocks, grid_class, neighbor):
     heights, window_dev, cols_dev, members, flattened = blocks.shape
-    half = lax.rem(lax.axis_index("layer"), 2)
-    native = jnp.transpose(blocks[:, 0], (0, 2, 1, 3))
-    away = lax.dynamic_slice_in_dim(native, (1 - half) * QH, QH, 2)
-    kept = lax.dynamic_slice_in_dim(native, half * QH, QH, 2)
-    layers = lax.axis_size("layer")
-    came = lax.ppermute(away, "layer", [(l, l ^ 1) for l in range(layers)])
+    native = jnp.transpose(blocks[:, 0], (0, 2, 1, 3)).reshape(TILES, cols_dev, flattened)
     mu, mask = tables(grid_class, neighbor)
-
-    own = blocks[0, 0]
-    cut = own.reshape(2, QH, PAIRS, 2, 4, NZ, 8)
-    cut = jnp.transpose(cut, (5, 0, 2, 1, 6, 3, 4)).reshape(layers, PAIRS, QH * 8, 2 * 4)
-    cut = lax.all_to_all(cut, "layer", split_axis=0, concat_axis=0, tiled=True)
-    cut = cut.reshape(layers, PAIRS, 2, QH * 4, 2, 4)
-    left = jnp.transpose(cut, (2, 1, 3, 4, 0, 5)).reshape(2, PAIRS, QH * 4, 128)
-
-    cubed = whole(mu, mask, kept.reshape(TILES, QH, 256), came.reshape(TILES, QH, 256), left)
-    cubed = cubed.reshape(2, members, 4, QH, BS)
+    cubed = whole(mu, mask, native).reshape(2, members, 4, QH, BS)
     cubed = jnp.transpose(cubed, (0, 3, 1, 2, 4)).reshape(cols_dev, members, flattened)
-    return (1.5 * own.astype(F32) - 0.5 * cubed).astype(BF16)[None]
+    return (1.5 * blocks[0, 0].astype(F32) - 0.5 * cubed).astype(BF16)[None]
 
 
 def solution(mesh):

time: 140 us -> 123 us (0.88)
  starting transfers between devices: 10.3 us -> 0 us
  local copies, waits for them, and re-layouts: 9.5 us -> 1.91 us
  Pallas kernels: 114 us -> 119 us
  waiting for transfers between devices: 3.78 us -> 0 us
    all_to_all x1 -> x0, starting transfers between devices: 8.29 us -> none  [per_device(): cut = lax.all_to_all(cut, 'layer', split_axis=0, concat_axis=0, tiled=True)]
    pallas_call x1, Pallas kernels: 110 us -> 115 us  [whole(): pl.pallas_call(whole_kernel, out_shape=jax.ShapeDtypeStruct((2, MEM, 4, Q...]
    all_to_all x1 -> x0, waiting for transfers between devices: 3.78 us -> none  [per_device(): cut = lax.all_to_all(cut, 'layer', split_axis=0, concat_axis=0, tiled=True)]
    dynamic_slice x1 -> x0, local copies, waits for them, and re-layouts: 2.67 us -> none  [per_device(): away = lax.dynamic_slice_in_dim(native, (1 - half) * QH, QH, 2)]
    another operation x2 -> x0, local copies, waits for them, and re-layouts: 2.44 us -> none  [per_device(): cut = own.reshape(2, QH, PAIRS, 2, 4, NZ, 8)]
    ppermute x1 -> x0, starting transfers between devices: 2.03 us -> none  [per_device(): came = lax.ppermute(away, 'layer', [(l, l ^ 1) for l in range(layers)])]
    reshape x3 -> x0, local copies, waits for them, and re-layouts: 1.97 us -> none  [the longest x1 0.99 us: per_device(): jnp.transpose(cut, (5, 0, 2, 1, 6, 3, 4))]
  transfers between devices with their start and end apart: 2 -> 0, of which waited for: 1 -> 0; matrix products, arithmetic and copies ran while one was open for 4% -> 0% of each run, Pallas kernels for 3% -> 0%
where the time goes in v3:
time: 123 us
  Pallas kernels  119 us (97%)
  other arithmetic  2.54 us (2%)
  local copies, waits for them, and re-layouts  1.91 us (2%)
    pallas_call x1, Pallas kernels, whole(): pl.pallas_call(whole_kernel, out_shape=jax.ShapeDtypeStruct((2, MEM, 4, Q...  115 us
    pallas_call x1, Pallas kernels, tables(): pl.pallas_call(tables_kernel, out_shape=(jax.ShapeDtypeStruct((MEM, NCLS)...  3.67 us

profile of v3, /device:TPU:1, one launch (start us, length us, event | category | flops | bytes accessed | tf_op | source)
XLA Modules:
  0.0 123.1 jit_solution(18248764925724668687)
XLA Ops:
  0.0 1.4 %copy.4.gcol_ref = s32[64,1]{1,0:T(8,128)} copy(s32[64,1]{0,1:T(1,128)} %bitcast.17) | data formatting | bytes 512 | tf_op jit(solution)/shard_map/broadcast_in_dim | solution.py:72
  1.4 3.7 %shard_map.37 = (s32[12,64]{1,0:T(8,128)}, f32[12,64,64]{2,1,0:T(8,128)}) custom-call(s32[64,1]{1,0:T(8,128)} %copy.4.gcol_ref, s32[12,64,64]{2,1,0:T(8,128)} %bitcast.16), custom_call_target="tpu_custom_call" | custom-call | tf_op jit(solution)/shard_map/pallas_call | solution.py:63
  5.0 114.9 %shard_map.38 = f32[2,12,4,512]{3,2,1,0:T(4,128)} custom-call(s32[12,64]{1,0:T(8,128)} %get-tuple-element.7.mu_ref, f32[12,64,64]{2,1,0:T(8,128)} %get-tuple-element.8.mask_ref, bf16[192,16,256]{2,1,0:T(8,128)(2,1)} %bitcast.14), custom_call_target="tpu_custom_call" | custom-call | tf_op jit(solution)/shard_map/pallas_call | solution.py:406
  120.0 1.0 broadcast_multiply_fusion
  120.9 0.2 mul.43
  121.1 0.1 copy.5
  121.2 0.3 mul.45
  121.5 1.6 %fusion = bf16[1,16,12,256]{3,1,2,0:T(8,128)(2,1)} fusion(f32[1,16,12,256]{3,1,2,0:T(8,128)S(1)} %mul.45, bf16[16,1,16,12,256]{4,2,3,1,0:T(8,128)(2,1)} %param.3), kind=kLoop, calls=%fused_computation.1 | loop fusion | flops 196608 | bytes 393216 | tf_op jit(solution)/shard_map/convert_element_type | solution.py:460
